TPU v7x, 32 devices: a whole 2x2x4 slice. The times are simulated.
32 devices in a mesh: fsdp: 32 (over z, y, x, core).
Axes of the slice: x: 2, y: 2, z: 4, core: 2. Of those that a mesh axis runs over, the one named last changes fastest.
Arguments:
- block_input: float32 [4096, 1024], P('fsdp'), may hold values from -12 to 12
- ln1_gain: bfloat16 [1024], P('fsdp'), may hold values from 0.5 to 1.5
- ln1_bias: bfloat16 [1024], P('fsdp'), may hold values from -3 to 3
- w_qkv: bfloat16 [1024, 3072], P('fsdp'), may hold values from -0.1875 to 0.1875
- bias_qv: bfloat16 [2048], P('fsdp'), may hold values from -3 to 3
- w_out: bfloat16 [1024, 1024], P('fsdp'), may hold values from -0.75 to 0.75
- bias_out: bfloat16 [1024], P('fsdp'), may hold values from -3 to 3
- ln2_gain: bfloat16 [1024], P('fsdp'), may hold values from 0.5 to 1.5
- ln2_bias: bfloat16 [1024], P('fsdp'), may hold values from -3 to 3
- w_fc: bfloat16 [1024, 4096], P('fsdp'), may hold values from -0.1875 to 0.1875
- bias_fc: bfloat16 [4096], P('fsdp'), may hold values from -3 to 3
- w_proj: bfloat16 [4096, 1024], P('fsdp'), may hold values from -0.09375 to 0.09375
- bias_proj: bfloat16 [1024], P('fsdp'), may hold values from -3 to 3
- seq_lengths: int32 [16], replicated, may hold values from 1 to 512, 4096 in all
- out_grad: float32 [4096, 1024], P('fsdp'), may hold values from -12 to 12
Outputs:
- block_output: float32 [4096, 1024], P('fsdp')
- grad_input: float32 [4096, 1024], P('fsdp')
- grad_ln1_gain: float32 [1024], P('fsdp')
- grad_ln1_bias: float32 [1024], P('fsdp')
- grad_w_qkv: float32 [1024, 3072], P('fsdp')
- grad_bias_qv: float32 [2048], P('fsdp')
- grad_w_out: float32 [1024, 1024], P('fsdp')
- grad_bias_out: float32 [1024], P('fsdp')
- grad_ln2_gain: float32 [1024], P('fsdp')
- grad_ln2_bias: float32 [1024], P('fsdp')
- grad_w_fc: float32 [1024, 4096], P('fsdp')
- grad_bias_fc: float32 [4096], P('fsdp')
- grad_w_proj: float32 [4096, 1024], P('fsdp')
- grad_bias_proj: float32 [1024], P('fsdp')
Inputs may be any that keep to these rules, and one draw needn't show every extreme that they name: `seq_lengths`: sequences lie end to end in token order: sequence s begins after the sum of the lengths before it. The lengths sum to 4096 and the largest is exactly 512.
All inputs are finite; a program needn't handle non-finite values.
Results may differ from a plain program's by a relative error of at most 0.0095.
Values may be sent and summed in bfloat16 or wider, within the bound.
No kernel may reach another device: no remote copies, remote signals or barrier semaphores. Data moves between devices by JAX's collectives and lax.ppermute only.
A program may use at most 256 MiB of HBM per device.

v0:
```python
import math

import jax
import jax.numpy as jnp
from jax import lax
from jax.experimental import pallas as pl
from jax.experimental.pallas import tpu as pltpu
from jax.sharding import PartitionSpec as P

HEADS = 16
HEAD_DIM = 64
REACH = 4
PLANE = 8
INTERPRET = False


EPSILON = 1e-05
GELU_C = math.sqrt(2.0 / math.pi)
MASKED = -1e30


def from_behind(value, axis, steps):
    count = lax.axis_size(axis)
    first, last = (max(0, -steps), min(count, count - steps))
    return lax.ppermute(value, axis, [(source, source + steps) for source in range(first, last)])


def layer_norm(values, gain, shift_bias):
    row_mean = jnp.mean(values, axis=-1, keepdims=True)
    centred = values - row_mean
    row_var = jnp.mean(centred * centred, axis=-1, keepdims=True)
    row_inverse = lax.rsqrt(row_var + EPSILON)
    normed = centred * row_inverse
    return (normed, row_inverse, normed * gain + shift_bias)


def norm_back(grad_normed, gain, normed, row_inverse):
    scaled = grad_normed * gain
    first_mean = jnp.mean(scaled, axis=-1, keepdims=True)
    second_mean = jnp.mean(scaled * normed, axis=-1, keepdims=True)
    return row_inverse * (scaled - first_mean - normed * second_mean)


def gelu_pair(inputs):
    inner_arg = GELU_C * (inputs + 0.044715 * inputs * inputs * inputs)
    tanh_value = jnp.tanh(inner_arg)
    activated = 0.5 * inputs * (1.0 + tanh_value)
    derivative = 0.5 * (1.0 + tanh_value) + 0.5 * inputs * (
        1.0 - tanh_value * tanh_value
    ) * GELU_C * (1.0 + 3.0 * 0.044715 * inputs * inputs)
    return (activated, derivative)


def attention_scores(query_heads, key_heads, query_pos, key_pos, token_start):
    scores = jnp.einsum(
        "qhd,khd->hqk", query_heads, key_heads, preferred_element_type=jnp.float32
    ) * HEAD_DIM ** (-0.5)
    visible = (key_pos[None, :] >= token_start[:, None]) & (key_pos[None, :] <= query_pos[:, None])
    return jnp.where(visible[None], scores, MASKED)


def local_any(
    block_input,
    ln1_gain,
    ln1_bias,
    w_qkv,
    bias_qv,
    w_out,
    bias_out,
    ln2_gain,
    ln2_bias,
    w_fc,
    bias_fc,
    w_proj,
    bias_proj,
    seq_lengths,
    out_grad,
):
    full = (
        lax.all_gather(ln1_gain, "fsdp", axis=0, tiled=True),
        lax.all_gather(ln1_bias, "fsdp", axis=0, tiled=True),
        lax.all_gather(w_qkv, "fsdp", axis=0, tiled=True),
        lax.all_gather(bias_qv, "fsdp", axis=0, tiled=True),
        lax.all_gather(w_out, "fsdp", axis=0, tiled=True),
        lax.all_gather(bias_out, "fsdp", axis=0, tiled=True),
        lax.all_gather(ln2_gain, "fsdp", axis=0, tiled=True),
        lax.all_gather(ln2_bias, "fsdp", axis=0, tiled=True),
        lax.all_gather(w_fc, "fsdp", axis=0, tiled=True),
        lax.all_gather(bias_fc, "fsdp", axis=0, tiled=True),
        lax.all_gather(w_proj, "fsdp", axis=0, tiled=True),
        lax.all_gather(bias_proj, "fsdp", axis=0, tiled=True),
    )
    rows = block_input.shape[0]
    width = block_input.shape[1]
    device = lax.axis_index("fsdp")
    positions = device * rows + jnp.arange(rows, dtype=jnp.int32)
    key_pos = (device - REACH) * rows + jnp.arange((REACH + 1) * rows, dtype=jnp.int32)
    seq_ends = jnp.cumsum(seq_lengths)
    seq_starts = seq_ends - seq_lengths
    token_start = jnp.max(
        jnp.where(seq_starts[None, :] <= positions[:, None], seq_starts[None, :], 0), axis=1
    )
    gain_one = full[0].astype(jnp.float32)
    normed_one, inverse_one, affine_one = layer_norm(
        block_input, gain_one, full[1].astype(jnp.float32)
    )
    act_one = affine_one.astype(jnp.bfloat16)
    qkv_bias = jnp.concatenate(
        [
            full[3][:width].astype(jnp.float32),
            jnp.zeros((width,), jnp.float32),
            full[3][width:].astype(jnp.float32),
        ]
    )
    qkv = (jnp.dot(act_one, full[2], preferred_element_type=jnp.float32) + qkv_bias).astype(
        jnp.bfloat16
    )
    queries = qkv[:, :width]
    kv_own = qkv[:, width:]
    earlier = []
    moving = kv_own
    for _ in range(REACH):
        moving = from_behind(moving, "fsdp", 1)
        earlier.append(moving)
    kv_all = jnp.concatenate(earlier[::-1] + [kv_own], axis=0)
    key_heads = kv_all[:, :width].reshape(-1, HEADS, HEAD_DIM)
    value_heads = kv_all[:, width:].reshape(-1, HEADS, HEAD_DIM)
    query_heads = queries.reshape(rows, HEADS, HEAD_DIM)
    scores = attention_scores(query_heads, key_heads, positions, key_pos, token_start)
    row_max = jnp.max(scores, axis=-1, keepdims=True)
    total = jnp.sum(jnp.exp(scores - row_max), axis=-1, keepdims=True)
    lse = row_max + jnp.log(total)
    attn_probs = jnp.exp(scores - lse).astype(jnp.bfloat16)
    mixed = (
        jnp.einsum("hqk,khd->qhd", attn_probs, value_heads, preferred_element_type=jnp.float32)
        .astype(jnp.bfloat16)
        .reshape(rows, width)
    )
    hidden_res = (
        block_input
        + jnp.dot(mixed, full[4], preferred_element_type=jnp.float32)
        + full[5].astype(jnp.float32)
    )
    gain_two = full[6].astype(jnp.float32)
    normed_two, inverse_two, affine_two = layer_norm(
        hidden_res, gain_two, full[7].astype(jnp.float32)
    )
    act_two = affine_two.astype(jnp.bfloat16)
    pre_act = jnp.dot(act_two, full[8], preferred_element_type=jnp.float32) + full[9].astype(
        jnp.float32
    )
    activated, derivative = gelu_pair(pre_act)
    gelu_out = activated.astype(jnp.bfloat16)
    block_output = (
        hidden_res
        + jnp.dot(gelu_out, full[10], preferred_element_type=jnp.float32)
        + full[11].astype(jnp.float32)
    )
    params_back = (
        lax.all_gather(ln1_gain, "fsdp", axis=0, tiled=True),
        lax.all_gather(ln1_bias, "fsdp", axis=0, tiled=True),
        lax.all_gather(w_qkv, "fsdp", axis=0, tiled=True),
        lax.all_gather(bias_qv, "fsdp", axis=0, tiled=True),
        lax.all_gather(w_out, "fsdp", axis=0, tiled=True),
        lax.all_gather(bias_out, "fsdp", axis=0, tiled=True),
        lax.all_gather(ln2_gain, "fsdp", axis=0, tiled=True),
        lax.all_gather(ln2_bias, "fsdp", axis=0, tiled=True),
        lax.all_gather(w_fc, "fsdp", axis=0, tiled=True),
        lax.all_gather(bias_fc, "fsdp", axis=0, tiled=True),
        lax.all_gather(w_proj, "fsdp", axis=0, tiled=True),
        lax.all_gather(bias_proj, "fsdp", axis=0, tiled=True),
    )
    grad_proj_bias = jnp.sum(out_grad, axis=0)
    out_grad_b = out_grad.astype(jnp.bfloat16)
    grad_proj_weight = jnp.dot(gelu_out.T, out_grad_b, preferred_element_type=jnp.float32)
    grad_pre = (
        jnp.dot(out_grad_b, params_back[10].T, preferred_element_type=jnp.float32) * derivative
    )
    grad_fc_bias = jnp.sum(grad_pre, axis=0)
    grad_pre_b = grad_pre.astype(jnp.bfloat16)
    grad_fc_weight = jnp.dot(act_two.T, grad_pre_b, preferred_element_type=jnp.float32)
    grad_act_two = jnp.dot(grad_pre_b, params_back[8].T, preferred_element_type=jnp.float32)
    grad_ln2_gain = jnp.sum(grad_act_two * normed_two, axis=0)
    grad_ln2_bias = jnp.sum(grad_act_two, axis=0)
    grad_hidden = out_grad + norm_back(
        grad_act_two, params_back[6].astype(jnp.float32), normed_two, inverse_two
    )
    grad_out_bias = jnp.sum(grad_hidden, axis=0)
    grad_hidden_b = grad_hidden.astype(jnp.bfloat16)
    grad_out_weight = jnp.dot(mixed.T, grad_hidden_b, preferred_element_type=jnp.float32)
    grad_mixed = jnp.dot(
        grad_hidden_b, params_back[4].T, preferred_element_type=jnp.float32
    ).astype(jnp.bfloat16)
    grad_heads = grad_mixed.reshape(rows, HEADS, HEAD_DIM)
    scores_again = attention_scores(query_heads, key_heads, positions, key_pos, token_start)
    probs_full = jnp.exp(scores_again - lse)
    probs_round = probs_full.astype(jnp.bfloat16)
    grad_probs = jnp.einsum(
        "qhd,khd->hqk", grad_heads, value_heads, preferred_element_type=jnp.float32
    )
    row_delta = jnp.sum(probs_full * grad_probs, axis=-1, keepdims=True)
    grad_scores = (probs_full * (grad_probs - row_delta) * HEAD_DIM ** (-0.5)).astype(jnp.bfloat16)
    grad_queries = jnp.einsum(
        "hqk,khd->qhd", grad_scores, key_heads, preferred_element_type=jnp.float32
    ).reshape(rows, width)
    grad_keys_all = jnp.einsum(
        "hqk,qhd->khd", grad_scores, query_heads, preferred_element_type=jnp.float32
    ).reshape(-1, width)
    grad_values_all = jnp.einsum(
        "hqk,qhd->khd", probs_round, grad_heads, preferred_element_type=jnp.float32
    ).reshape(-1, width)
    grad_kv_all = jnp.concatenate([grad_keys_all, grad_values_all], axis=1)
    pieces = [
        grad_kv_all[(REACH - distance) * rows : (REACH - distance + 1) * rows]
        for distance in range(REACH + 1)
    ]
    grad_kv = pieces[REACH]
    for distance in range(REACH - 1, -1, -1):
        grad_kv = from_behind(grad_kv, "fsdp", -1) + pieces[distance]
    grad_qv_bias = jnp.concatenate(
        [jnp.sum(grad_queries, axis=0), jnp.sum(grad_kv[:, width:], axis=0)]
    )
    grad_qkv = jnp.concatenate([grad_queries, grad_kv], axis=1).astype(jnp.bfloat16)
    grad_qkv_weight = jnp.dot(act_one.T, grad_qkv, preferred_element_type=jnp.float32)
    grad_act_one = jnp.dot(grad_qkv, params_back[2].T, preferred_element_type=jnp.float32)
    grad_ln1_gain = jnp.sum(grad_act_one * normed_one, axis=0)
    grad_ln1_bias = jnp.sum(grad_act_one, axis=0)
    grad_input = grad_hidden + norm_back(
        grad_act_one, params_back[0].astype(jnp.float32), normed_one, inverse_one
    )
    reduced = tuple(
        (
            lax.psum_scatter(grad_ln1_gain, "fsdp", scatter_dimension=0, tiled=True),
            lax.psum_scatter(grad_ln1_bias, "fsdp", scatter_dimension=0, tiled=True),
            lax.psum_scatter(grad_qkv_weight, "fsdp", scatter_dimension=0, tiled=True),
            lax.psum_scatter(grad_qv_bias, "fsdp", scatter_dimension=0, tiled=True),
            lax.psum_scatter(grad_out_weight, "fsdp", scatter_dimension=0, tiled=True),
            lax.psum_scatter(grad_out_bias, "fsdp", scatter_dimension=0, tiled=True),
            lax.psum_scatter(grad_ln2_gain, "fsdp", scatter_dimension=0, tiled=True),
            lax.psum_scatter(grad_ln2_bias, "fsdp", scatter_dimension=0, tiled=True),
            lax.psum_scatter(grad_fc_weight, "fsdp", scatter_dimension=0, tiled=True),
            lax.psum_scatter(grad_fc_bias, "fsdp", scatter_dimension=0, tiled=True),
            lax.psum_scatter(grad_proj_weight, "fsdp", scatter_dimension=0, tiled=True),
            lax.psum_scatter(grad_proj_bias, "fsdp", scatter_dimension=0, tiled=True),
        )
    )
    return (block_output, grad_input) + reduced


BF = jnp.bfloat16
F32 = jnp.float32
AXIS = "fsdp"


def mm(a, b):
    return jnp.dot(a, b, preferred_element_type=F32)


def mm_nt(a, b):
    return lax.dot_general(a, b, (((1,), (1,)), ((), ())), preferred_element_type=F32)


def mm_tn(a, b):
    return lax.dot_general(a, b, (((0,), (0,)), ((), ())), preferred_element_type=F32)


def pick(array, index):
    return lax.dynamic_index_in_dim(array, index, 0, keepdims=False)


def swap(value, mask):
    count = lax.axis_size(AXIS)
    return lax.ppermute(value, AXIS, [(d, d ^ mask) for d in range(count)])


def add_everywhere(terms):
    step = 1
    while step < lax.axis_size(AXIS):
        terms = terms + swap(terms, step)
        step *= 2
    return terms


def chip_groups():
    count = lax.axis_size(AXIS)
    return [
        [first + core + f for f in range(0, PLANE, 2)]
        for first in range(0, count, PLANE)
        for core in (0, 1)
    ]


def over_chips(blocks):
    return lax.all_to_all(blocks, AXIS, 0, 0, axis_index_groups=chip_groups(), tiled=True)


def plane_gather(value):
    mine = over_chips(jnp.broadcast_to(value[None], (PLANE // 2,) + value.shape))
    return (mine, swap(mine, 1))


def halves(rows):
    return [half.reshape(-1, half.shape[-1]) for half in rows]


def core_fold(mine, other):
    arrived = swap(other.astype(BF), 1).astype(F32)
    return (mine + arrived).astype(BF).reshape(PLANE // 2, -1, mine.shape[-1])


def chip_fold(kept):
    return jnp.sum(over_chips(kept).astype(F32), axis=0)


def plane_groups():
    count = lax.axis_size(AXIS)
    return [[first + f for f in range(PLANE)] for first in range(0, count, PLANE)]


def z_groups():
    count = lax.axis_size(AXIS)
    return [[first + f for first in range(0, count, PLANE)] for f in range(PLANE)]


def plane_exchange(blocks):
    return lax.all_to_all(blocks, AXIS, 0, 0, axis_index_groups=plane_groups(), tiled=True)


def z_gather(value):
    return lax.all_gather(value, AXIS, axis_index_groups=z_groups(), axis=0, tiled=True)


def z_reduce(partial):
    return lax.psum_scatter(
        partial.astype(BF), AXIS, axis_index_groups=z_groups(), scatter_dimension=0, tiled=True
    )


def after(value, earlier):
    return lax.optimization_barrier((value, earlier))[0]


def key_block(core, u):
    side = (u & 1) ^ core
    return jnp.where(u >= 0, (u >> 1) + 4 * side, PLANE + ((u + 8) >> 1) - 2 + 2 * side)


def masked_pair(rows):
    lane = lax.broadcasted_iota(jnp.int32, rows.shape, 1)
    zero = jnp.zeros_like(rows)
    first = lane < HEAD_DIM
    return jnp.concatenate([jnp.where(first, rows, zero), jnp.where(first, zero, rows)], 0)


def unpair(both, rows):
    lane = lax.broadcasted_iota(jnp.int32, (rows, both.shape[1]), 1)
    return jnp.where(lane < HEAD_DIM, both[:rows], both[rows:])


def block_probs(core, b, qkv_ref, kv_ref, start_ref):
    rows = qkv_ref.shape[1]
    t = 2 * (b & 3) + (core ^ (b >> 2))
    scaled = (qkv_ref[b, :, 0:128].astype(F32) * HEAD_DIM ** (-0.5)).astype(BF)
    q2 = masked_pair(scaled)
    start = start_ref[b]
    lane = lax.broadcasted_iota(jnp.int32, (rows, 128), 1)
    row = lax.broadcasted_iota(jnp.int32, (rows, 128), 0)
    tiles = []
    places = []
    for j in range(REACH + 1):
        u = t - REACH + j
        at = key_block(core, u)
        places.append(at)
        key_pos = u * 128 + lane
        visible = (key_pos >= start) & (key_pos <= t * 128 + row)
        visible = jnp.concatenate([visible, visible], 0)
        tiles.append(jnp.where(visible, mm_nt(q2, kv_ref[at, :, 0:128]), MASKED))
    scores = jnp.concatenate(tiles, 1)
    top = jnp.max(scores, axis=-1, keepdims=True)
    weights = jnp.exp(scores - top)
    total = jnp.sum(weights, axis=-1, keepdims=True)
    return (places, q2, weights * (1.0 / total))


def attend_kernel(core_ref, qkv_ref, kv_ref, start_ref, out_ref):
    core = core_ref[0]
    rows = qkv_ref.shape[1]

    def body(b, carry):
        places, _, probs = block_probs(core, b, qkv_ref, kv_ref, start_ref)
        probs_b = probs.astype(BF)
        both = jnp.zeros((2 * rows, 128), F32)
        for j, at in enumerate(places):
            both = both + mm(probs_b[:, j * 128 : (j + 1) * 128], kv_ref[at, :, 128:256])
        out_ref[b] = unpair(both, rows).astype(BF)
        return carry

    lax.fori_loop(0, PLANE, body, 0)


def attend_back_kernel(core_ref, qkv_ref, kv_ref, start_ref, grad_ref, dq_ref, dkv_ref):
    core = core_ref[0]
    rows = qkv_ref.shape[1]
    dkv_ref[...] = jnp.zeros_like(dkv_ref)

    def body(b, carry):
        places, q2, probs = block_probs(core, b, qkv_ref, kv_ref, start_ref)
        g2 = masked_pair(grad_ref[b])
        grad_probs = jnp.concatenate(
            [mm_nt(g2, kv_ref[at, :, 128:256]) for at in places], 1
        )
        delta = jnp.sum(probs * grad_probs, axis=-1, keepdims=True)
        grad_scores = (probs * (grad_probs - delta)).astype(BF)
        probs_b = probs.astype(BF)
        both = jnp.zeros((2 * rows, 128), F32)
        for j, at in enumerate(places):
            part = grad_scores[:, j * 128 : (j + 1) * 128]
            both = both + mm(part, kv_ref[at, :, 0:128])
            dkv_ref[at, :, 0:128] += mm_tn(part, q2)
            dkv_ref[at, :, 128:256] += mm_tn(probs_b[:, j * 128 : (j + 1) * 128], g2)
        dq_ref[b] = unpair(both, rows) * HEAD_DIM ** (-0.5)
        return carry

    lax.fori_loop(0, PLANE, body, 0)


def vmem_call(kernel, outs, args):
    return pl.pallas_call(
        kernel,
        out_shape=outs,
        in_specs=[pl.BlockSpec(memory_space=pltpu.SMEM)]
        + [pl.BlockSpec(memory_space=pltpu.VMEM)] * (len(args) - 1),
        out_specs=[pl.BlockSpec(memory_space=pltpu.VMEM)] * len(outs),
        interpret=INTERPRET,
    )(*args)


def local_plane(
    block_input,
    ln1_gain,
    ln1_bias,
    w_qkv,
    bias_qv,
    w_out,
    bias_out,
    ln2_gain,
    ln2_bias,
    w_fc,
    bias_fc,
    w_proj,
    bias_proj,
    seq_lengths,
    out_grad,
):
    count = lax.axis_size(AXIS)
    planes = count // PLANE
    device = lax.axis_index(AXIS)
    z = device // PLANE
    f = device % PLANE
    core = device & 1
    rows, width = block_input.shape
    tokens = PLANE * rows
    share = width // count
    part = width // PLANE
    core_scalar = core.astype(jnp.int32).reshape(1)

    vectors = [ln1_gain, ln1_bias, bias_out, ln2_gain, ln2_bias, bias_proj, bias_qv, bias_fc]
    packed = jnp.concatenate([vector.astype(F32) for vector in vectors]).astype(BF)
    lanes = packed.shape[0]
    qkv_blocks = w_qkv.reshape(share, 3, PLANE, part).transpose(2, 0, 1, 3)
    fc_blocks = w_fc.reshape(share, planes, PLANE, -1).transpose(2, 0, 1, 3)
    hidden = planes * fc_blocks.shape[3]
    slices = jnp.concatenate(
        [
            qkv_blocks.reshape(PLANE, share, 3 * part),
            fc_blocks.reshape(PLANE, share, hidden),
        ],
        axis=2,
    )
    extra = jnp.pad(packed.reshape(1, 1, lanes), ((0, 0), (0, 7), (0, slices.shape[2] - lanes)))
    extra = jnp.broadcast_to(extra, (PLANE, 8, slices.shape[2]))
    arrived = plane_exchange(jnp.concatenate([slices, extra], axis=1))

    row_mean = jnp.mean(block_input, axis=-1, keepdims=True)
    centred = block_input - row_mean
    inverse_one = lax.rsqrt(jnp.mean(centred * centred, axis=-1, keepdims=True) + EPSILON)
    normed_one = centred * inverse_one
    normed_all = plane_gather(normed_one.astype(BF))

    first = z_gather(arrived[:, :, : 3 * part].reshape(-1, 3 * part))
    first = first.reshape(count, share + 8, 3 * part)
    w_qkv_all = first[:, :share].reshape(width, 3 * part)
    vectors = first[:, share, :lanes]

    w_out_column = z_gather(w_out).reshape(planes, share, width)
    og_all = lax.all_gather(
        after(out_grad.astype(BF), w_qkv_all),
        AXIS,
        axis_index_groups=plane_groups(),
        axis=0,
        tiled=True,
    ).reshape(PLANE // 2, 2, rows, width)
    w_fc_here = arrived[:, :share, 3 * part :].reshape(PLANE * share, hidden)
    w_fc_all = z_gather(after(w_fc_here, w_qkv_all))

    def whole(i):
        return vectors[:, i * share : (i + 1) * share].reshape(width).astype(F32)

    gain_one, shift_one, b_out, gain_two, shift_two, b_proj = [whole(i) for i in range(6)]
    qv_at = 6 * share
    fc_at = qv_at + bias_qv.shape[0]
    b_qv = vectors[:, qv_at:fc_at].reshape(2, PLANE, part)
    b_qv = lax.dynamic_index_in_dim(b_qv, f, 1, keepdims=False).astype(F32)
    b_fc = vectors[:, fc_at:].reshape(planes, PLANE, -1)
    b_fc = lax.dynamic_index_in_dim(b_fc, f, 1, keepdims=False).reshape(-1).astype(F32)
    b_qkv = jnp.concatenate([b_qv[0], jnp.zeros((part,), F32), b_qv[1]])

    act_one = [
        (half.astype(F32) * gain_one + shift_one).astype(BF) for half in halves(normed_all)
    ]
    qkv = jnp.concatenate([(mm(half, w_qkv_all) + b_qkv).astype(BF) for half in act_one])
    qkv = qkv.reshape(PLANE, rows, 3 * part)
    kv_own = qkv[:, :, part:]
    kv_late = kv_own.reshape(2, 4, rows, 2 * part)[:, 2:].reshape(4, rows, 2 * part)
    kv_before = from_behind(kv_late, AXIS, PLANE)
    kv_all = jnp.concatenate([kv_own, kv_before])
    block = jnp.arange(PLANE, dtype=jnp.int32)
    order = 2 * (block & 3) + (core ^ (block >> 2))
    positions = (z * tokens + order * rows)[:, None] + jnp.arange(rows, dtype=jnp.int32)[None]
    seq_starts = jnp.cumsum(seq_lengths) - seq_lengths
    token_start = jnp.max(
        jnp.where(seq_starts <= positions[:, :, None], seq_starts, 0), axis=2, keepdims=True
    )
    begins = (token_start - z * tokens).astype(jnp.int32)
    w_proj_all = z_gather(after(w_proj, qkv))
    w_out_column = after(w_out_column, qkv)
    w_out_all = plane_exchange(jnp.repeat(w_out_column, 2, axis=0))
    w_out_all = lax.dynamic_slice_in_dim(w_out_all, 4 * core, 4, 0).reshape(part, width)
    (mixed,) = vmem_call(
        attend_kernel,
        [jax.ShapeDtypeStruct((PLANE, rows, part), BF)],
        (core_scalar, qkv, kv_all, begins),
    )
    mixed = halves((mixed[:4], mixed[4:]))
    out_sum = chip_fold(core_fold(*[mm(half, w_out_all) for half in mixed]))
    hidden_res = block_input + out_sum + b_out
    normed_two, inverse_two, affine_two = layer_norm(hidden_res, gain_two, shift_two)
    act_two = halves(plane_gather(affine_two.astype(BF)))
    og = [
        lax.dynamic_index_in_dim(og_all, side, 1, keepdims=False).reshape(-1, width)
        for side in (core, 1 - core)
    ]
    pairs = [gelu_pair(mm(half, w_fc_all) + b_fc) for half in act_two]
    gelu_out = [activated.astype(BF) for activated, _ in pairs]

    grad_pre = [mm_nt(half, w_proj_all) * pair[1] for half, pair in zip(og, pairs)]
    grad_pre_b = [half.astype(BF) for half in grad_pre]
    partial_two = [mm_nt(half, w_fc_all) for half in grad_pre_b]
    gelu_late, pre_late, act_late, partial_two = lax.optimization_barrier(
        (gelu_out, grad_pre_b, act_two, partial_two)
    )
    kept_two = core_fold(*partial_two)
    grad_act_two = chip_fold(kept_two)
    fc_part = (mm_tn(act_late[0], pre_late[0]) + mm_tn(act_late[1], pre_late[1])).astype(BF)
    proj_part = (mm_tn(gelu_late[0], og[0]) + mm_tn(gelu_late[1], og[1])).astype(BF)
    grad_w_fc_here = z_reduce(fc_part)
    grad_w_proj = z_reduce(proj_part).astype(F32)
    proj_terms = [mm(half, w_proj_all) for half in gelu_late]
    kept_proj = core_fold(*proj_terms)
    grad_fc_bias = jnp.sum(grad_pre[0], axis=0) + jnp.sum(grad_pre[1], axis=0)
    grad_hidden = out_grad + norm_back(grad_act_two, gain_two, normed_two, inverse_two)
    grad_hidden_b = halves(plane_gather(grad_hidden.astype(BF)))
    grad_mixed = jnp.concatenate([mm_nt(half, w_out_all).astype(BF) for half in grad_hidden_b])
    grad_mixed, fc_part, proj_part, kept_proj = lax.optimization_barrier(
        (grad_mixed, fc_part, proj_part, kept_proj)
    )
    grad_mixed = grad_mixed.reshape(PLANE, rows, part)
    proj_sum = chip_fold(kept_proj)
    block_output = hidden_res + proj_sum + b_proj

    grad_queries, grad_kv_all = vmem_call(
        attend_back_kernel,
        [
            jax.ShapeDtypeStruct((PLANE, rows, part), F32),
            jax.ShapeDtypeStruct((PLANE + 4, rows, 2 * part), F32),
        ],
        (core_scalar, qkv, kv_all, begins, grad_mixed),
    )
    kv_back = from_behind(grad_kv_all[PLANE:].astype(BF), AXIS, -PLANE).astype(F32)
    grad_kv = grad_kv_all[:PLANE].reshape(2, 4, rows, 2 * part)
    kv_back = jnp.pad(kv_back.reshape(2, 2, rows, 2 * part), ((0, 0), (2, 0), (0, 0), (0, 0)))
    grad_kv = (grad_kv + kv_back).reshape(tokens, 2 * part)
    grad_queries = grad_queries.reshape(tokens, part)
    grad_qkv = jnp.concatenate([grad_queries, grad_kv], axis=1)
    qkv_sums = jnp.sum(grad_qkv, axis=0)
    grad_qkv = grad_qkv.astype(BF)
    grad_qkv = [grad_qkv[: tokens // 2], grad_qkv[tokens // 2 :]]
    qkv_part = (mm_tn(act_one[0], grad_qkv[0]) + mm_tn(act_one[1], grad_qkv[1])).astype(BF)
    grad_w_qkv_here = z_reduce(qkv_part)
    grad_qkv = after(grad_qkv, qkv_part)
    partial_one = [mm_nt(half, w_qkv_all) for half in grad_qkv]
    kept_one = core_fold(*partial_one)
    grad_act_one = chip_fold(kept_one)

    mixed = after(mixed, grad_queries)
    out_part = mm_tn(mixed[0], grad_hidden_b[0]) + mm_tn(mixed[1], grad_hidden_b[1])
    out_part = jnp.tile(out_part.astype(BF).reshape((4,) + w_out.shape), (2, 1, 1))
    out_part = plane_exchange(out_part).reshape((4, 2) + w_out.shape)
    out_part = lax.dynamic_index_in_dim(out_part, f // 4, 1, keepdims=False)
    grad_w_out = z_reduce(out_part.reshape(width // PLANE, width))

    leaving = jnp.concatenate([grad_w_qkv_here, grad_w_fc_here], axis=1)
    landed = plane_exchange(leaving.reshape(PLANE, share, 3 * part + hidden))
    grad_w_out = after(grad_w_out, landed).astype(F32)
    landed = landed.astype(F32)
    grad_w_qkv = landed[:, :, : 3 * part].reshape(PLANE, share, 3, part)
    grad_w_qkv = grad_w_qkv.transpose(1, 2, 0, 3).reshape(w_qkv.shape)
    grad_w_fc = landed[:, :, 3 * part :].reshape(PLANE, share, planes, -1)
    grad_w_fc = grad_w_fc.transpose(1, 2, 0, 3).reshape(w_fc.shape)

    grad_input = grad_hidden + norm_back(grad_act_one, gain_one, normed_one, inverse_one)

    normed_halves = [half.astype(F32) for half in halves(normed_all)]
    sums = [
        jnp.sum(partial_one[0] * normed_halves[0], axis=0)
        + jnp.sum(partial_one[1] * normed_halves[1], axis=0),
        jnp.sum(partial_one[0], axis=0) + jnp.sum(partial_one[1], axis=0),
        jnp.sum(grad_hidden, axis=0),
        jnp.sum(grad_act_two * normed_two, axis=0),
        jnp.sum(grad_act_two, axis=0),
        jnp.sum(out_grad, axis=0),
    ]
    qv_sums = jnp.stack([qkv_sums[:part], qkv_sums[2 * part :]])
    here = (jnp.arange(width, dtype=jnp.int32) // part == f)[None]
    qv_terms = jnp.where(here, jnp.tile(qv_sums, (1, PLANE)), 0.0)
    fc_terms = jnp.where(here, jnp.tile(grad_fc_bias.reshape(planes, part), (1, PLANE)), 0.0)
    terms = jnp.concatenate([jnp.stack(sums), qv_terms, fc_terms])
    total = add_everywhere(terms)
    small = pick(total[:6].reshape(6, count, share).transpose(1, 0, 2), device)
    small_qv = pick(total[6:8].reshape(count, -1), device)
    small_fc = pick(total[8:].reshape(count, -1), device)
    return (
        block_output,
        grad_input,
        small[0],
        small[1],
        grad_w_qkv,
        small_qv,
        grad_w_out,
        small[2],
        small[3],
        small[4],
        grad_w_fc,
        small_fc,
        grad_w_proj,
        small[5],
    )


def solution(mesh):
    if mesh.size != 32:
        return planned(mesh, local_any)
    return planned(mesh, local_plane)


def planned(mesh, local):
    return jax.shard_map(
        local,
        mesh=mesh,
        in_specs=(
            P("fsdp", None),
            P("fsdp"),
            P("fsdp"),
            P("fsdp", None),
            P("fsdp"),
            P("fsdp", None),
            P("fsdp"),
            P("fsdp"),
            P("fsdp"),
            P("fsdp", None),
            P("fsdp"),
            P("fsdp", None),
            P("fsdp"),
            P(),
            P("fsdp", None),
        ),
        out_specs=(
            P("fsdp", None),
            P("fsdp", None),
            P("fsdp"),
            P("fsdp"),
            P("fsdp", None),
            P("fsdp"),
            P("fsdp", None),
            P("fsdp"),
            P("fsdp"),
            P("fsdp"),
            P("fsdp", None),
            P("fsdp"),
            P("fsdp", None),
            P("fsdp"),
        ),
        check_vma=False,
    )
```

profile of v0, /device:TPU:0, one launch (start us, length us, event | category | flops | bytes accessed | tf_op | source)
XLA Modules:
  0.0 328.3 jit_solution(17882864358205827103)
XLA Ops:
  11.4 5.2 %all-to-all-start.1 = ((bf16[8,40,896]{2,1,0:T(8,128)(2,1)}), bf16[8,40,896]{2,1,0:T(8,128)(2,1)S(1)}, u32[]{:S(2)}, u32[]{:S(2)}) async-start(bf16[8,40,896]{2,1,0:T(8,128)(2,1)} %pad_maximum_fusion.3), calls=%async_computation.1 | async-start | bytes 1146880 | tf_op jit(solution)/shard_map/all_to_all | solution.py:326
  17.1 9.7 %all-to-all-done.1 = bf16[8,40,896]{2,1,0:T(8,128)(2,1)S(1)} async-done(((bf16[8,40,896]{2,1,0:T(8,128)(2,1)}), bf16[8,40,896]{2,1,0:T(8,128)(2,1)S(1)}, u32[]{:S(2)}, u32[]{:S(2)}) %all-to-all-start.1) | async-done | bytes 573472 | tf_op jit(solution)/shard_map/all_to_all | solution.py:326
  28.1 3.5 %all-to-all-start = ((bf16[4,128,1024]{2,1,0:T(8,128)(2,1)}), bf16[4,128,1024]{2,1,0:T(8,128)(2,1)S(1)}, u32[]{:S(2)}, u32[]{:S(2)}) async-start(bf16[4,128,1024]{2,1,0:T(8,128)(2,1)} %broadcast_in_dim.36), calls=%async_computation | async-start | bytes 2097152 | tf_op jit(solution)/shard_map/all_to_all | solution.py:294
  32.5 21.7 %all_gather.15 = bf16[1280,384]{1,0:T(8,128)(2,1)S(1)} all-gather(bf16[320,384]{1,0:T(8,128)(2,1)S(1)} %bitcast.231), channel_id=1, replica_groups={{0,8,16,24},{1,9,17,25},{2,10,18,26},{3,11,19,27},{4,12,20,28},{5,13,21..., dimensions={0}, use_global_device_ids=true | all-gather | bytes 1228800 | tf_op jit(solution)/shard_map/all_gather | solution.py:330
  63.7 16.5 %all_gather.16 = bf16[128,1024]{1,0:T(8,128)(2,1)S(1)} all-gather(bf16[32,1024]{1,0:T(8,128)(2,1)S(1)} %copy-done.25), channel_id=1, replica_groups={{0,8,16,24},{1,9,17,25},{2,10,18,26},{3,11,19,27},{4,12,20,28},{5,13,21..., dimensions={0}, use_global_device_ids=true | all-gather | bytes 327680 | tf_op jit(solution)/shard_map/all_gather | solution.py:330
  81.1 3.9 %all-to-all-start.2 = ((bf16[8,32,1024]{2,1,0:T(8,128)(2,1)}), bf16[8,32,1024]{2,1,0:T(8,128)(2,1)S(1)}, u32[]{:S(2)}, u32[]{:S(2)}) async-start(bf16[8,32,1024]{2,1,0:T(8,128)(2,1)} %bitcast.26), calls=%async_computation.2 | async-start | bytes 1048576 | tf_op jit(solution)/shard_map/all_to_all | solution.py:326
  88.0 8.6 %shard_map.254 = bf16[8,128,128]{2,1,0:T(8,128)(2,1)} custom-call(s32[1]{0:T(128)} %bitcast.core_ref, bf16[8,128,384]{2,1,0:T(8,128)(2,1)} %bitcast.186, bf16[12,128,256]{2,1,0:T(8,128)(2,1)} %pad_maximum_fusion.2.kv_ref, s32[8,128,1]{2,1,0:T(8,128)} %copy.48.start_ref), custom_call_target="tpu_custom_call" | custom-call | tf_op jit(solution)/shard_map/pallas_call | solution.py:428
  103.6 4.1 %all-to-all-start.3 = ((bf16[4,128,1024]{2,1,0:T(8,128)(2,1)}), bf16[4,128,1024]{2,1,0:T(8,128)(2,1)S(1)}, u32[]{:S(2)}, u32[]{:S(2)}) async-start(bf16[4,128,1024]{2,1,0:T(8,128)(2,1)} %bitcast.201), calls=%async_computation.3 | async-start | bytes 2097152 | tf_op jit(solution)/shard_map/all_to_all | solution.py:294
  109.1 12.5 %all-to-all-done.3 = bf16[4,128,1024]{2,1,0:T(8,128)(2,1)S(1)} async-done(((bf16[4,128,1024]{2,1,0:T(8,128)(2,1)}), bf16[4,128,1024]{2,1,0:T(8,128)(2,1)S(1)}, u32[]{:S(2)}, u32[]{:S(2)}) %all-to-all-start.3) | async-done | bytes 1048608 | tf_op jit(solution)/shard_map/all_to_all | solution.py:294
  124.5 4.4 %all-to-all-start.4 = ((bf16[4,128,1024]{2,1,0:T(8,128)(2,1)}), bf16[4,128,1024]{2,1,0:T(8,128)(2,1)}, u32[]{:S(2)}, u32[]{:S(2)}) async-start(bf16[4,128,1024]{2,1,0:T(8,128)(2,1)} %broadcast_in_dim.42), calls=%async_computation.4 | async-start | bytes 2097152 | tf_op jit(solution)/shard_map/all_to_all | solution.py:294
  130.2 11.8 %all-to-all-done.4 = bf16[4,128,1024]{2,1,0:T(8,128)(2,1)} async-done(((bf16[4,128,1024]{2,1,0:T(8,128)(2,1)}), bf16[4,128,1024]{2,1,0:T(8,128)(2,1)}, u32[]{:S(2)}, u32[]{:S(2)}) %all-to-all-start.4) | async-done | bytes 1048608 | tf_op jit(solution)/shard_map/all_to_all | solution.py:294
  145.0 3.6 %multiply_convert_fusion.1 = (bf16[512,512]{1,0:T(8,128)(2,1)}, f32[512,512]{1,0:T(8,128)}) fusion(f32[512]{0:T(512)} %bitcast.246, bf16[512,1024]{1,0:T(8,128)(2,1)} %bitcast.30, bf16[1024,512]{1,0:T(8,128)(2,1)} %all-gather.4.cloned.1.call-done), kind=kOutput, calls=%fused_computation.61 | convolution fusion | flops 539492352 | bytes 3672064 | tf_op jit(solution)/shard_map/dot_general | solution.py:256
  148.6 10.3 %all-gather.8.cloned.1.call-done = bf16[512,1024]{1,0:T(8,128)(2,1)} async-done(((bf16[128,1024]{1,0:T(8,128)(2,1)}), bf16[512,1024]{1,0:T(8,128)(2,1)}) %all-gather.8.cloned.1.call-update) | async-done | bytes 1048592 | tf_op jit(solution)/shard_map/all_gather | solution.py:330
  158.9 3.8 %fusion.42 = (f32[512]{0:T(512)}, bf16[512,512]{1,0:T(8,128)(2,1)S(1)}) fusion(f32[512,512]{1,0:T(8,128)} %get-tuple-element.106, bf16[512,1024]{1,0:T(8,128)(2,1)} %bitcast.198, bf16[512,1024]{1,0:T(8,128)(2,1)} %all-gather.8.cloned.1.call-done), kind=kOutput, calls=%fused_computation.154 | convolution fusion | flops 542113280 | bytes 3672064 | tf_op jit(solution)/shard_map/dot_general | solution.py:260
  163.4 3.1 multiply_convert_fusion
  173.1 4.2 %all-to-all-start.5 = ((bf16[4,128,1024]{2,1,0:T(8,128)(2,1)}), bf16[4,128,1024]{2,1,0:T(8,128)(2,1)}, u32[]{:S(2)}, u32[]{:S(2)}) async-start(bf16[4,128,1024]{2,1,0:T(8,128)(2,1)} %bitcast.202), calls=%async_computation.5 | async-start | bytes 2097152 | tf_op jit(solution)/shard_map/all_to_all | solution.py:294
  183.1 8.5 %all-to-all-done.5 = bf16[4,128,1024]{2,1,0:T(8,128)(2,1)} async-done(((bf16[4,128,1024]{2,1,0:T(8,128)(2,1)}), bf16[4,128,1024]{2,1,0:T(8,128)(2,1)}, u32[]{:S(2)}, u32[]{:S(2)}) %all-to-all-start.5) | async-done | bytes 1048608 | tf_op jit(solution)/shard_map/all_to_all | solution.py:294
  197.7 3.5 %all-to-all-start.6 = ((bf16[4,128,1024]{2,1,0:T(8,128)(2,1)}), bf16[4,128,1024]{2,1,0:T(8,128)(2,1)S(1)}, u32[]{:S(2)}, u32[]{:S(2)}) async-start(bf16[4,128,1024]{2,1,0:T(8,128)(2,1)} %broadcast_in_dim.43), calls=%async_computation.6 | async-start | bytes 2097152 | tf_op jit(solution)/shard_map/all_to_all | solution.py:294
  201.5 3.1 convolution_convert_fusion.1
  209.7 4.8 %all-to-all-done.6 = bf16[4,128,1024]{2,1,0:T(8,128)(2,1)S(1)} async-done(((bf16[4,128,1024]{2,1,0:T(8,128)(2,1)}), bf16[4,128,1024]{2,1,0:T(8,128)(2,1)S(1)}, u32[]{:S(2)}, u32[]{:S(2)}) %all-to-all-start.6) | async-done | bytes 1048608 | tf_op jit(solution)/shard_map/all_to_all | solution.py:294
  216.5 3.4 %add_convert_fusion.1 = bf16[512,1024]{1,0:T(8,128)(2,1)} fusion(bf16[512,1024]{1,0:T(8,128)(2,1)} %collective-permute-done.6, bf16[512,512]{1,0:T(8,128)(2,1)} %get-tuple-element.45, bf16[512,1024]{1,0:T(8,128)(2,1)} %all-gather.8.cloned.1.call-done), kind=kOutput, calls=%fused_computation.21 | convolution fusion | flops 538443776 | bytes 3670016 | tf_op jit(solution)/shard_map/dot_general | solution.py:256
  222.8 11.4 %shard_map.255 = (f32[8,128,128]{2,1,0:T(8,128)}, f32[12,128,256]{2,1,0:T(8,128)}) custom-call(s32[1]{0:T(128)} %bitcast.core_ref, bf16[8,128,384]{2,1,0:T(8,128)(2,1)} %bitcast.187, bf16[12,128,256]{2,1,0:T(8,128)(2,1)} %pad_maximum_fusion.2.kv_ref, s32[8,128,1]{2,1,0:T(8,128)} %copy.48.start_ref, bf16[8,128,128]{2,1,0:T(8,128)(2,1)} %bitcast.222), custom_call_target="tpu_custom_call" | custom-call | tf_op jit(solution)/shard_map/pallas_call | solution.py:428
  242.3 4.1 %all-to-all-start.10 = ((bf16[8,32,1024]{2,1,0:T(8,128)(2,1)}), bf16[8,32,1024]{2,1,0:T(8,128)(2,1)}, u32[]{:S(2)}, u32[]{:S(2)}) async-start(bf16[8,32,1024]{2,1,0:T(8,128)(2,1)} %bitcast.66), calls=%async_computation.12 | async-start | bytes 1048576 | tf_op jit(solution)/shard_map/all_to_all | solution.py:326
  255.2 3.4 %fusion.37 = (f32[1024]{0:T(1024)S(1)}, f32[1024]{0:T(1024)S(1)}, bf16[512,1024]{1,0:T(8,128)(2,1)}) fusion(bf16[4,128,1024]{2,1,0:T(8,128)(2,1)} %copy-done.6, bf16[512,384]{1,0:T(8,128)(2,1)} %get-tuple-element.52, bf16[1024,384]{1,0:T(8,128)(2,1)} %bitcast.208), kind=kOutput, calls=%fused_computation.149 | convolution fusion | flops 405272576 | bytes 3284992 | tf_op jit(solution)/shard_map/dot_general | solution.py:260
  258.9 3.3 %fusion.50 = f32[512,1024]{1,0:T(8,128)} fusion(bf16[512,384]{1,0:T(8,128)(2,1)} %get-tuple-element.51, bf16[1024,384]{1,0:T(8,128)(2,1)} %bitcast.209), kind=kOutput, calls=%fused_computation.162 | convolution fusion | flops 402653184 | bytes 3276800 | tf_op jit(solution)/shard_map/dot_general | solution.py:260
  262.2 3.5 %all-to-all-start.7 = ((bf16[4,128,1024]{2,1,0:T(8,128)(2,1)}), bf16[4,128,1024]{2,1,0:T(8,128)(2,1)S(1)}, u32[]{:S(2)}, u32[]{:S(2)}) async-start(bf16[4,128,1024]{2,1,0:T(8,128)(2,1)} %bitcast.225), calls=%async_computation.7 | async-start | bytes 2097152 | tf_op jit(solution)/shard_map/all_to_all | solution.py:294
  265.9 3.4 %fusion.38 = (f32[1024]{0:T(1024)S(1)}, f32[1024]{0:T(1024)S(1)}, bf16[512,1024]{1,0:T(8,128)(2,1)}) fusion(f32[512,1024]{1,0:T(8,128)} %fusion.50, bf16[4,128,1024]{2,1,0:T(8,128)(2,1)S(1)} %all-to-all-done, bf16[512,1024]{1,0:T(8,128)(2,1)} %collective-permute-done.8), kind=kLoop, calls=%fused_computation.150 | loop fusion | flops 3667968 | bytes 5251072 | tf_op jit(solution)/shard_map/reduce_sum | solution.py:627
  274.6 7.1 %collective-permute-done.10 = f32[12,1024]{1,0:T(8,128)S(1)} collective-permute-done((f32[12,1024]{1,0:T(8,128)S(1)}, f32[12,1024]{1,0:T(8,128)S(1)}, u32[]{:S(2)}, u32[]{:S(2)}) %collective-permute-start.10) | collective-permute-done | bytes 49184 | tf_op jit(solution)/shard_map/ppermute | solution.py:273
  288.6 3.6 %all-to-all-start.8 = ((bf16[4,128,1024]{2,1,0:T(8,128)(2,1)}), bf16[4,128,1024]{2,1,0:T(8,128)(2,1)S(1)}, u32[]{:S(2)}, u32[]{:S(2)}) async-start(bf16[4,128,1024]{2,1,0:T(8,128)(2,1)} %bitcast.49), calls=%async_computation.8 | async-start | bytes 2097152 | tf_op jit(solution)/shard_map/all_to_all | solution.py:294
  294.6 4.8 %collective-permute-done.13 = f32[12,1024]{1,0:T(8,128)S(1)} collective-permute-done((f32[12,1024]{1,0:T(8,128)S(1)}, f32[12,1024]{1,0:T(8,128)S(1)}, u32[]{:S(2)}, u32[]{:S(2)}) %collective-permute-start.13) | collective-permute-done | bytes 49184 | tf_op jit(solution)/shard_map/ppermute | solution.py:273
  304.6 3.5 %all-to-all-start.9 = ((bf16[8,32,896]{2,1,0:T(8,128)(2,1)}), bf16[8,32,896]{2,1,0:T(8,128)(2,1)S(1)}, u32[]{:S(2)}, u32[]{:S(2)}) async-start(bf16[8,32,896]{2,1,0:T(8,128)(2,1)} %bitcast.62), calls=%async_computation.11 | async-start | bytes 917504 | tf_op jit(solution)/shard_map/all_to_all | solution.py:326
  309.5 7.5 %all-to-all-done.9 = bf16[8,32,896]{2,1,0:T(8,128)(2,1)S(1)} async-done(((bf16[8,32,896]{2,1,0:T(8,128)(2,1)}), bf16[8,32,896]{2,1,0:T(8,128)(2,1)S(1)}, u32[]{:S(2)}, u32[]{:S(2)}) %all-to-all-start.9) | async-done | bytes 458784 | tf_op jit(solution)/shard_map/all_to_all | solution.py:326
  (283 shorter events, 107.0 us)
Async XLA Ops:
  11.4 15.4 %all-to-all-start.1 = ((bf16[8,40,896]{2,1,0:T(8,128)(2,1)}), bf16[8,40,896]{2,1,0:T(8,128)(2,1)S(1)}, u32[]{:S(2)}, u32[]{:S(2)}) async-start(bf16[8,40,896]{2,1,0:T(8,128)(2,1)} %pad_maximum_fusion.3), calls=%async_computation.1 | async-start | bytes 1146880 | tf_op jit(solution)/shard_map/all_to_all | solution.py:326
  28.1 27.1 %all-to-all-start = ((bf16[4,128,1024]{2,1,0:T(8,128)(2,1)}), bf16[4,128,1024]{2,1,0:T(8,128)(2,1)S(1)}, u32[]{:S(2)}, u32[]{:S(2)}) async-start(bf16[4,128,1024]{2,1,0:T(8,128)(2,1)} %broadcast_in_dim.36), calls=%async_computation | async-start | bytes 2097152 | tf_op jit(solution)/shard_map/all_to_all | solution.py:294
  31.6 110.5 %all-gather.6.cloned.1.call-start = ((), (), s32[]{:S(2)}) async-start(), calls=%async_computation.16 | async-start | bytes 2359296 | tf_op jit(solution)/shard_map/all_gather | solution.py:496
  55.2 3.1 collective-permute-start
  61.7 24.4 %collective-permute-start.1 = (bf16[4,128,256]{2,1,0:T(8,128)(2,1)}, bf16[4,128,256]{2,1,0:T(8,128)(2,1)}, u32[]{:S(2)}, u32[]{:S(2)}) collective-permute-start(bf16[4,128,256]{2,1,0:T(8,128)(2,1)} %bitcast.21), channel_id=1, source_target_pairs={{0,8},{1,9},{2,10},{3,11},{4,12},{5,13},{6,14},{7,15},{8,16},{9,17... | collective-permute-start | bytes 786440 | tf_op jit(solution)/shard_map/ppermute | solution.py:25
  81.1 16.6 %all-to-all-start.2 = ((bf16[8,32,1024]{2,1,0:T(8,128)(2,1)}), bf16[8,32,1024]{2,1,0:T(8,128)(2,1)S(1)}, u32[]{:S(2)}, u32[]{:S(2)}) async-start(bf16[8,32,1024]{2,1,0:T(8,128)(2,1)} %bitcast.26), calls=%async_computation.2 | async-start | bytes 1048576 | tf_op jit(solution)/shard_map/all_to_all | solution.py:326
  85.0 60.0 %all-gather.4.cloned.1.call-start = ((), (), s32[]{:S(2)}) async-start(), calls=%async_computation.15 | async-start | bytes 1310720 | tf_op jit(solution)/shard_map/all_gather | solution.py:330
  99.2 3.0 collective-permute-start.2
  103.6 18.0 %all-to-all-start.3 = ((bf16[4,128,1024]{2,1,0:T(8,128)(2,1)}), bf16[4,128,1024]{2,1,0:T(8,128)(2,1)S(1)}, u32[]{:S(2)}, u32[]{:S(2)}) async-start(bf16[4,128,1024]{2,1,0:T(8,128)(2,1)} %bitcast.201), calls=%async_computation.3 | async-start | bytes 2097152 | tf_op jit(solution)/shard_map/all_to_all | solution.py:294
  107.6 51.2 %all-gather.8.cloned.1.call-start = ((), (), s32[]{:S(2)}) async-start(), calls=%async_computation.17 | async-start | bytes 1310720 | tf_op jit(solution)/shard_map/all_gather | solution.py:330
  124.5 17.6 %all-to-all-start.4 = ((bf16[4,128,1024]{2,1,0:T(8,128)(2,1)}), bf16[4,128,1024]{2,1,0:T(8,128)(2,1)}, u32[]{:S(2)}, u32[]{:S(2)}) async-start(bf16[4,128,1024]{2,1,0:T(8,128)(2,1)} %broadcast_in_dim.42), calls=%async_computation.4 | async-start | bytes 2097152 | tf_op jit(solution)/shard_map/all_to_all | solution.py:294
  142.1 21.3 %collective-permute-start.3 = (bf16[4,128,1024]{2,1,0:T(8,128)(2,1)}, bf16[4,128,1024]{2,1,0:T(8,128)(2,1)}, u32[]{:S(2)}, u32[]{:S(2)}) collective-permute-start(bf16[4,128,1024]{2,1,0:T(8,128)(2,1)} %all-to-all-done.4), channel_id=1, source_target_pairs={{0,1},{1,0},{2,3},{3,2},{4,5},{5,4},{6,7},{7,6},{8,9},{9,8},{10,11... | collective-permute-start | bytes 3145736 | tf_op jit(solution)/shard_map/ppermute | solution.py:273
  169.1 2.7 collective-permute-start.4
  173.1 18.5 %all-to-all-start.5 = ((bf16[4,128,1024]{2,1,0:T(8,128)(2,1)}), bf16[4,128,1024]{2,1,0:T(8,128)(2,1)}, u32[]{:S(2)}, u32[]{:S(2)}) async-start(bf16[4,128,1024]{2,1,0:T(8,128)(2,1)} %bitcast.202), calls=%async_computation.5 | async-start | bytes 2097152 | tf_op jit(solution)/shard_map/all_to_all | solution.py:294
  177.4 95.5 %reduce-scatter.11.cloned.1.call-start = ((), (), s32[]{:S(2)}) async-start(), calls=%async_computation.21 | async-start | bytes 1310720 | tf_op jit(solution)/shard_map/reduce_scatter | solution.py:334
  197.7 16.9 %all-to-all-start.6 = ((bf16[4,128,1024]{2,1,0:T(8,128)(2,1)}), bf16[4,128,1024]{2,1,0:T(8,128)(2,1)S(1)}, u32[]{:S(2)}, u32[]{:S(2)}) async-start(bf16[4,128,1024]{2,1,0:T(8,128)(2,1)} %broadcast_in_dim.43), calls=%async_computation.6 | async-start | bytes 2097152 | tf_op jit(solution)/shard_map/all_to_all | solution.py:294
  201.2 100.0 %reduce-scatter.7.cloned.1.call-start = ((), (), s32[]{:S(2)}) async-start(), calls=%async_computation.19 | async-start | bytes 1310720 | tf_op jit(solution)/shard_map/reduce_scatter | solution.py:334
  204.6 12.0 %collective-permute-start.6 = (bf16[512,1024]{1,0:T(8,128)(2,1)}, bf16[512,1024]{1,0:T(8,128)(2,1)}, u32[]{:S(2)}, u32[]{:S(2)}) collective-permute-start(bf16[512,1024]{1,0:T(8,128)(2,1)} %convolution_convert_fusion.1), channel_id=1, source_target_pairs={{0,1},{1,0},{2,3},{3,2},{4,5},{5,4},{6,7},{7,6},{8,9},{9,8},{10,11... | collective-permute-start | bytes 3145736 | tf_op jit(solution)/shard_map/ppermute | solution.py:273
  214.5 5.8 %collective-permute-start.5 = (bf16[4,128,1024]{2,1,0:T(8,128)(2,1)S(1)}, bf16[4,128,1024]{2,1,0:T(8,128)(2,1)}, u32[]{:S(2)}, u32[]{:S(2)}) collective-permute-start(bf16[4,128,1024]{2,1,0:T(8,128)(2,1)S(1)} %all-to-all-done.6), channel_id=1, source_target_pairs={{0,1},{1,0},{2,3},{3,2},{4,5},{5,4},{6,7},{7,6},{8,9},{9,8},{10,11... | collective-permute-start | bytes 3145736 | tf_op jit(solution)/shard_map/ppermute | solution.py:273
  238.3 10.9 %collective-permute-start.7 = (bf16[4,128,256]{2,1,0:T(8,128)(2,1)}, bf16[4,128,256]{2,1,0:T(8,128)(2,1)}, u32[]{:S(2)}, u32[]{:S(2)}) collective-permute-start(bf16[4,128,256]{2,1,0:T(8,128)(2,1)} %slice.203), channel_id=1, source_target_pairs={{8,0},{9,1},{10,2},{11,3},{12,4},{13,5},{14,6},{15,7},{16,8},{17,9... | collective-permute-start | bytes 786440 | tf_op jit(solution)/shard_map/ppermute | solution.py:25
  242.3 19.9 %all-to-all-start.10 = ((bf16[8,32,1024]{2,1,0:T(8,128)(2,1)}), bf16[8,32,1024]{2,1,0:T(8,128)(2,1)}, u32[]{:S(2)}, u32[]{:S(2)}) async-start(bf16[8,32,1024]{2,1,0:T(8,128)(2,1)} %bitcast.66), calls=%async_computation.12 | async-start | bytes 1048576 | tf_op jit(solution)/shard_map/all_to_all | solution.py:326
  246.5 54.7 %reduce-scatter.5.cloned.1.call-start = ((), (), s32[]{:S(2)}) async-start(), calls=%async_computation.18 | async-start | bytes 983040 | tf_op jit(solution)/shard_map/reduce_scatter | solution.py:334
  258.6 7.3 %collective-permute-start.8 = (bf16[512,1024]{1,0:T(8,128)(2,1)}, bf16[512,1024]{1,0:T(8,128)(2,1)}, u32[]{:S(2)}, u32[]{:S(2)}) collective-permute-start(bf16[512,1024]{1,0:T(8,128)(2,1)} %get-tuple-element.71), channel_id=1, source_target_pairs={{0,1},{1,0},{2,3},{3,2},{4,5},{5,4},{6,7},{7,6},{8,9},{9,8},{10,11... | collective-permute-start | bytes 3145736 | tf_op jit(solution)/shard_map/ppermute | solution.py:273
  262.2 25.4 %all-to-all-start.7 = ((bf16[4,128,1024]{2,1,0:T(8,128)(2,1)}), bf16[4,128,1024]{2,1,0:T(8,128)(2,1)S(1)}, u32[]{:S(2)}, u32[]{:S(2)}) async-start(bf16[4,128,1024]{2,1,0:T(8,128)(2,1)} %bitcast.225), calls=%async_computation.7 | async-start | bytes 2097152 | tf_op jit(solution)/shard_map/all_to_all | solution.py:294
  265.8 52.5 %reduce-scatter.9.cloned.1.call-start = ((), (), s32[]{:S(2)}) async-start(), calls=%async_computation.20 | async-start | bytes 327680 | tf_op jit(solution)/shard_map/reduce_scatter | solution.py:334
  269.4 1.5 collective-permute-start.9
  270.9 10.8 %collective-permute-start.10 = (f32[12,1024]{1,0:T(8,128)S(1)}, f32[12,1024]{1,0:T(8,128)S(1)}, u32[]{:S(2)}, u32[]{:S(2)}) collective-permute-start(f32[12,1024]{1,0:T(8,128)S(1)} %add.349), channel_id=1, source_target_pairs={{0,2},{1,3},{2,0},{3,1},{4,6},{5,7},{6,4},{7,5},{8,10},{9,11},{10,... | collective-permute-start | bytes 147464 | tf_op jit(solution)/shard_map/ppermute | solution.py:273
  281.8 4.3 %collective-permute-start.11 = (f32[12,1024]{1,0:T(8,128)S(1)}, f32[12,1024]{1,0:T(8,128)S(1)}, u32[]{:S(2)}, u32[]{:S(2)}) collective-permute-start(f32[12,1024]{1,0:T(8,128)S(1)} %add.350), channel_id=1, source_target_pairs={{0,4},{1,5},{2,6},{3,7},{4,0},{5,1},{6,2},{7,3},{8,12},{9,13},{10,... | collective-permute-start | bytes 147464 | tf_op jit(solution)/shard_map/ppermute | solution.py:273
  286.1 6.2 %collective-permute-start.12 = (f32[12,1024]{1,0:T(8,128)S(1)}, f32[12,1024]{1,0:T(8,128)S(1)}, u32[]{:S(2)}, u32[]{:S(2)}) collective-permute-start(f32[12,1024]{1,0:T(8,128)S(1)} %add.351), channel_id=1, source_target_pairs={{0,8},{1,9},{2,10},{3,11},{4,12},{5,13},{6,14},{7,15},{8,0},{9,1},... | collective-permute-start | bytes 147464 | tf_op jit(solution)/shard_map/ppermute | solution.py:273
  288.6 15.9 %all-to-all-start.8 = ((bf16[4,128,1024]{2,1,0:T(8,128)(2,1)}), bf16[4,128,1024]{2,1,0:T(8,128)(2,1)S(1)}, u32[]{:S(2)}, u32[]{:S(2)}) async-start(bf16[4,128,1024]{2,1,0:T(8,128)(2,1)} %bitcast.49), calls=%async_computation.8 | async-start | bytes 2097152 | tf_op jit(solution)/shard_map/all_to_all | solution.py:294
  292.3 7.1 %collective-permute-start.13 = (f32[12,1024]{1,0:T(8,128)S(1)}, f32[12,1024]{1,0:T(8,128)S(1)}, u32[]{:S(2)}, u32[]{:S(2)}) collective-permute-start(f32[12,1024]{1,0:T(8,128)S(1)} %add.352), channel_id=1, source_target_pairs={{0,16},{1,17},{2,18},{3,19},{4,20},{5,21},{6,22},{7,23},{8,24},{9,... | collective-permute-start | bytes 147464 | tf_op jit(solution)/shard_map/ppermute | solution.py:273
  304.6 12.4 %all-to-all-start.9 = ((bf16[8,32,896]{2,1,0:T(8,128)(2,1)}), bf16[8,32,896]{2,1,0:T(8,128)(2,1)S(1)}, u32[]{:S(2)}, u32[]{:S(2)}) async-start(bf16[8,32,896]{2,1,0:T(8,128)(2,1)} %bitcast.62), calls=%async_computation.11 | async-start | bytes 917504 | tf_op jit(solution)/shard_map/all_to_all | solution.py:326
  (46 other events, 272.1 us)
Sparse Core Ops, SparseCore 0:
  55.4 26.8 all-gather.5
  101.4 28.3 all-gather.3
  131.4 27.3 all-gather.7
  181.2 27.0 reduce-scatter.10
  215.4 25.9 reduce-scatter.6
  259.0 23.2 reduce-scatter.4
  285.1 19.3 reduce-scatter.8
where the time goes:
time: 330 us; the launch traced here: 328 us
  waiting for transfers between devices  86.3 us (26%)
  starting transfers between devices  54.9 us (17%)
  matrix products  46.4 us (14%)
  blocking collectives  38.2 us (12%)
  local copies, waits for them, and re-layouts  34.3 us (10%)
  other arithmetic  33.1 us (10%)
  Pallas kernels  20 us (6%)
  between operations  15.1 us (5%)
    all_to_all x7, waiting for transfers between devices, over_chips(): lax.all_to_all(blocks, AXIS, 0, 0, axis_index_groups=chip_groups(), tiled...  39.2 us
    all_gather x2, blocking collectives, z_gather(): lax.all_gather(value, AXIS, axis_index_groups=z_groups(), axis=0, tiled=T...  38.2 us
    all_to_all x7, starting transfers between devices, over_chips(): lax.all_to_all(blocks, AXIS, 0, 0, axis_index_groups=chip_groups(), tiled...  26.9 us
    pallas_call x2, Pallas kernels, vmem_call(): pl.pallas_call(kernel, out_shape=outs, in_specs=[pl.BlockSpec(memory_spac...  20 us
    dot_general x8, matrix products, mm(): return jnp.dot(a, b, preferred_element_type=F32)  17.5 us
    all_to_all x4, waiting for transfers between devices, plane_exchange(): lax.all_to_all(blocks, AXIS, 0, 0, axis_index_groups=plane_groups(), tile...  17.2 us
    ppermute x12, waiting for transfers between devices, swap(): return lax.ppermute(value, AXIS, [(d, d ^ mask) for d in range(count)])  16.8 us
    all_to_all x4, starting transfers between devices, plane_exchange(): lax.all_to_all(blocks, AXIS, 0, 0, axis_index_groups=plane_groups(), tile...  16.7 us
  transfers between devices with their start and end apart: 32, of which 15 were waited for; matrix products, arithmetic and copies ran while one was open for 29% of the time, Pallas kernels for 6%

commit v1 on v0

--- a/solution.py
+++ b/solution.py
@@ -12,6 +12,7 @@
 REACH = 4
 PLANE = 8
 INTERPRET = False
+AXIS = "fsdp"
 
 
 EPSILON = 1e-05
@@ -77,22 +78,22 @@
     out_grad,
 ):
     full = (
-        lax.all_gather(ln1_gain, "fsdp", axis=0, tiled=True),
-        lax.all_gather(ln1_bias, "fsdp", axis=0, tiled=True),
-        lax.all_gather(w_qkv, "fsdp", axis=0, tiled=True),
-        lax.all_gather(bias_qv, "fsdp", axis=0, tiled=True),
-        lax.all_gather(w_out, "fsdp", axis=0, tiled=True),
-        lax.all_gather(bias_out, "fsdp", axis=0, tiled=True),
-        lax.all_gather(ln2_gain, "fsdp", axis=0, tiled=True),
-        lax.all_gather(ln2_bias, "fsdp", axis=0, tiled=True),
-        lax.all_gather(w_fc, "fsdp", axis=0, tiled=True),
-        lax.all_gather(bias_fc, "fsdp", axis=0, tiled=True),
-        lax.all_gather(w_proj, "fsdp", axis=0, tiled=True),
-        lax.all_gather(bias_proj, "fsdp", axis=0, tiled=True),
+        lax.all_gather(ln1_gain, AXIS, axis=0, tiled=True),
+        lax.all_gather(ln1_bias, AXIS, axis=0, tiled=True),
+        lax.all_gather(w_qkv, AXIS, axis=0, tiled=True),
+        lax.all_gather(bias_qv, AXIS, axis=0, tiled=True),
+        lax.all_gather(w_out, AXIS, axis=0, tiled=True),
+        lax.all_gather(bias_out, AXIS, axis=0, tiled=True),
+        lax.all_gather(ln2_gain, AXIS, axis=0, tiled=True),
+        lax.all_gather(ln2_bias, AXIS, axis=0, tiled=True),
+        lax.all_gather(w_fc, AXIS, axis=0, tiled=True),
+        lax.all_gather(bias_fc, AXIS, axis=0, tiled=True),
+        lax.all_gather(w_proj, AXIS, axis=0, tiled=True),
+        lax.all_gather(bias_proj, AXIS, axis=0, tiled=True),
     )
     rows = block_input.shape[0]
     width = block_input.shape[1]
-    device = lax.axis_index("fsdp")
+    device = lax.axis_index(AXIS)
     positions = device * rows + jnp.arange(rows, dtype=jnp.int32)
     key_pos = (device - REACH) * rows + jnp.arange((REACH + 1) * rows, dtype=jnp.int32)
     seq_ends = jnp.cumsum(seq_lengths)
@@ -120,7 +121,7 @@
     earlier = []
     moving = kv_own
     for _ in range(REACH):
-        moving = from_behind(moving, "fsdp", 1)
+        moving = from_behind(moving, AXIS, 1)
         earlier.append(moving)
     kv_all = jnp.concatenate(earlier[::-1] + [kv_own], axis=0)
     key_heads = kv_all[:, :width].reshape(-1, HEADS, HEAD_DIM)
@@ -157,18 +158,18 @@
         + full[11].astype(jnp.float32)
     )
     params_back = (
-        lax.all_gather(ln1_gain, "fsdp", axis=0, tiled=True),
-        lax.all_gather(ln1_bias, "fsdp", axis=0, tiled=True),
-        lax.all_gather(w_qkv, "fsdp", axis=0, tiled=True),
-        lax.all_gather(bias_qv, "fsdp", axis=0, tiled=True),
-        lax.all_gather(w_out, "fsdp", axis=0, tiled=True),
-        lax.all_gather(bias_out, "fsdp", axis=0, tiled=True),
-        lax.all_gather(ln2_gain, "fsdp", axis=0, tiled=True),
-        lax.all_gather(ln2_bias, "fsdp", axis=0, tiled=True),
-        lax.all_gather(w_fc, "fsdp", axis=0, tiled=True),
-        lax.all_gather(bias_fc, "fsdp", axis=0, tiled=True),
-        lax.all_gather(w_proj, "fsdp", axis=0, tiled=True),
-        lax.all_gather(bias_proj, "fsdp", axis=0, tiled=True),
+        lax.all_gather(ln1_gain, AXIS, axis=0, tiled=True),
+        lax.all_gather(ln1_bias, AXIS, axis=0, tiled=True),
+        lax.all_gather(w_qkv, AXIS, axis=0, tiled=True),
+        lax.all_gather(bias_qv, AXIS, axis=0, tiled=True),
+        lax.all_gather(w_out, AXIS, axis=0, tiled=True),
+        lax.all_gather(bias_out, AXIS, axis=0, tiled=True),
+        lax.all_gather(ln2_gain, AXIS, axis=0, tiled=True),
+        lax.all_gather(ln2_bias, AXIS, axis=0, tiled=True),
+        lax.all_gather(w_fc, AXIS, axis=0, tiled=True),
+        lax.all_gather(bias_fc, AXIS, axis=0, tiled=True),
+        lax.all_gather(w_proj, AXIS, axis=0, tiled=True),
+        lax.all_gather(bias_proj, AXIS, axis=0, tiled=True),
     )
     grad_proj_bias = jnp.sum(out_grad, axis=0)
     out_grad_b = out_grad.astype(jnp.bfloat16)
@@ -216,7 +217,7 @@
     ]
     grad_kv = pieces[REACH]
     for distance in range(REACH - 1, -1, -1):
-        grad_kv = from_behind(grad_kv, "fsdp", -1) + pieces[distance]
+        grad_kv = from_behind(grad_kv, AXIS, -1) + pieces[distance]
     grad_qv_bias = jnp.concatenate(
         [jnp.sum(grad_queries, axis=0), jnp.sum(grad_kv[:, width:], axis=0)]
     )
@@ -230,18 +231,18 @@
     )
     reduced = tuple(
         (
-            lax.psum_scatter(grad_ln1_gain, "fsdp", scatter_dimension=0, tiled=True),
-            lax.psum_scatter(grad_ln1_bias, "fsdp", scatter_dimension=0, tiled=True),
-            lax.psum_scatter(grad_qkv_weight, "fsdp", scatter_dimension=0, tiled=True),
-            lax.psum_scatter(grad_qv_bias, "fsdp", scatter_dimension=0, tiled=True),
-            lax.psum_scatter(grad_out_weight, "fsdp", scatter_dimension=0, tiled=True),
-            lax.psum_scatter(grad_out_bias, "fsdp", scatter_dimension=0, tiled=True),
-            lax.psum_scatter(grad_ln2_gain, "fsdp", scatter_dimension=0, tiled=True),
-            lax.psum_scatter(grad_ln2_bias, "fsdp", scatter_dimension=0, tiled=True),
-            lax.psum_scatter(grad_fc_weight, "fsdp", scatter_dimension=0, tiled=True),
-            lax.psum_scatter(grad_fc_bias, "fsdp", scatter_dimension=0, tiled=True),
-            lax.psum_scatter(grad_proj_weight, "fsdp", scatter_dimension=0, tiled=True),
-            lax.psum_scatter(grad_proj_bias, "fsdp", scatter_dimension=0, tiled=True),
+            lax.psum_scatter(grad_ln1_gain, AXIS, scatter_dimension=0, tiled=True),
+            lax.psum_scatter(grad_ln1_bias, AXIS, scatter_dimension=0, tiled=True),
+            lax.psum_scatter(grad_qkv_weight, AXIS, scatter_dimension=0, tiled=True),
+            lax.psum_scatter(grad_qv_bias, AXIS, scatter_dimension=0, tiled=True),
+            lax.psum_scatter(grad_out_weight, AXIS, scatter_dimension=0, tiled=True),
+            lax.psum_scatter(grad_out_bias, AXIS, scatter_dimension=0, tiled=True),
+            lax.psum_scatter(grad_ln2_gain, AXIS, scatter_dimension=0, tiled=True),
+            lax.psum_scatter(grad_ln2_bias, AXIS, scatter_dimension=0, tiled=True),
+            lax.psum_scatter(grad_fc_weight, AXIS, scatter_dimension=0, tiled=True),
+            lax.psum_scatter(grad_fc_bias, AXIS, scatter_dimension=0, tiled=True),
+            lax.psum_scatter(grad_proj_weight, AXIS, scatter_dimension=0, tiled=True),
+            lax.psum_scatter(grad_proj_bias, AXIS, scatter_dimension=0, tiled=True),
         )
     )
     return (block_output, grad_input) + reduced
@@ -249,7 +250,6 @@
 
 BF = jnp.bfloat16
 F32 = jnp.float32
-AXIS = "fsdp"
 
 
 def mm(a, b):
@@ -494,7 +494,7 @@
 
     w_out_column = z_gather(w_out).reshape(planes, share, width)
     og_all = lax.all_gather(
-        after(out_grad.astype(BF), w_qkv_all),
+        after(out_grad.astype(BF), arrived),
         AXIS,
         axis_index_groups=plane_groups(),
         axis=0,
@@ -668,37 +668,37 @@
         local,
         mesh=mesh,
         in_specs=(
-            P("fsdp", None),
-            P("fsdp"),
-            P("fsdp"),
-            P("fsdp", None),
-            P("fsdp"),
-            P("fsdp", None),
-            P("fsdp"),
-            P("fsdp"),
-            P("fsdp"),
-            P("fsdp", None),
-            P("fsdp"),
-            P("fsdp", None),
-            P("fsdp"),
+            P(AXIS, None),
+            P(AXIS),
+            P(AXIS),
+            P(AXIS, None),
+            P(AXIS),
+            P(AXIS, None),
+            P(AXIS),
+            P(AXIS),
+            P(AXIS),
+            P(AXIS, None),
+            P(AXIS),
+            P(AXIS, None),
+            P(AXIS),
             P(),
-            P("fsdp", None),
+            P(AXIS, None),
         ),
         out_specs=(
-            P("fsdp", None),
-            P("fsdp", None),
-            P("fsdp"),
-            P("fsdp"),
-            P("fsdp", None),
-            P("fsdp"),
-            P("fsdp", None),
-            P("fsdp"),
-            P("fsdp"),
-            P("fsdp"),
-            P("fsdp", None),
-            P("fsdp"),
-            P("fsdp", None),
-            P("fsdp"),
+            P(AXIS, None),
+            P(AXIS, None),
+            P(AXIS),
+            P(AXIS),
+            P(AXIS, None),
+            P(AXIS),
+            P(AXIS, None),
+            P(AXIS),
+            P(AXIS),
+            P(AXIS),
+            P(AXIS, None),
+            P(AXIS),
+            P(AXIS, None),
+            P(AXIS),
         ),
         check_vma=False,
     )

time: 330 us -> 337 us (1.021)
  waiting for transfers between devices: 86.3 us -> 101 us
  local copies, waits for them, and re-layouts: 34.3 us -> 27.7 us
    all_to_all x7, waiting for transfers between devices: 39.2 us -> 52.8 us  [over_chips(): lax.all_to_all(blocks, AXIS, 0, 0, axis_index_groups=chip_groups(), tiled...]
    unnamed x99 -> x109, local copies, waits for them, and re-layouts: 7.13 us -> 3.13 us
  transfers between devices with their start and end apart: 32 -> 32, of which waited for: 15 -> 16; matrix products, arithmetic and copies ran while one was open for 29% -> 28% of each run, Pallas kernels for 6% -> 6%
where the time goes in v1:
time: 337 us; the launch traced here: 335 us
  waiting for transfers between devices  101 us (30%)
  starting transfers between devices  55.6 us (16%)
  matrix products  46.9 us (14%)
  blocking collectives  35.2 us (10%)
  other arithmetic  33.5 us (10%)
  local copies, waits for them, and re-layouts  27.7 us (8%)
  Pallas kernels  20.1 us (6%)
  between operations  15.3 us (5%)
    all_to_all x7, waiting for transfers between devices, over_chips(): lax.all_to_all(blocks, AXIS, 0, 0, axis_index_groups=chip_groups(), tiled...  52.8 us
    all_gather x2, blocking collectives, z_gather(): lax.all_gather(value, AXIS, axis_index_groups=z_groups(), axis=0, tiled=T...  35.2 us
    all_to_all x7, starting transfers between devices, over_chips(): lax.all_to_all(blocks, AXIS, 0, 0, axis_index_groups=chip_groups(), tiled...  28.9 us
    pallas_call x2, Pallas kernels, vmem_call(): pl.pallas_call(kernel, out_shape=outs, in_specs=[pl.BlockSpec(memory_spac...  20.1 us
    dot_general x8, matrix products, mm(): return jnp.dot(a, b, preferred_element_type=F32)  18.7 us
    ppermute x12, waiting for transfers between devices, swap(): return lax.ppermute(value, AXIS, [(d, d ^ mask) for d in range(count)])  18.6 us
    all_to_all x4, waiting for transfers between devices, plane_exchange(): lax.all_to_all(blocks, AXIS, 0, 0, axis_index_groups=plane_groups(), tile...  15.7 us
    dot_general x8, matrix products, mm_nt(): lax.dot_general(a, b, (((1,), (1,)), ((), ())), preferred_element_type=F32)  15.3 us
  transfers between devices with their start and end apart: 32, of which 16 were waited for; matrix products, arithmetic and copies ran while one was open for 28% of the time, Pallas kernels for 6%

profile of v1, /device:TPU:0, one launch (start us, length us, event | category | flops | bytes accessed | tf_op | source)
XLA Modules:
  0.0 334.9 jit_solution(3442325330167358545)
XLA Ops:
  12.5 5.3 %all-to-all-start = ((bf16[4,128,1024]{2,1,0:T(8,128)(2,1)}), bf16[4,128,1024]{2,1,0:T(8,128)(2,1)S(1)}, u32[]{:S(2)}, u32[]{:S(2)}) async-start(bf16[4,128,1024]{2,1,0:T(8,128)(2,1)} %broadcast_in_dim.36), calls=%async_computation | async-start | bytes 2097152 | tf_op jit(solution)/shard_map/all_to_all | solution.py:294
  19.9 11.6 %all-to-all-done = bf16[4,128,1024]{2,1,0:T(8,128)(2,1)S(1)} async-done(((bf16[4,128,1024]{2,1,0:T(8,128)(2,1)}), bf16[4,128,1024]{2,1,0:T(8,128)(2,1)S(1)}, u32[]{:S(2)}, u32[]{:S(2)}) %all-to-all-start) | async-done | bytes 1048608 | tf_op jit(solution)/shard_map/all_to_all | solution.py:294
  31.5 3.5 %all-to-all-start.1 = ((bf16[8,40,896]{2,1,0:T(8,128)(2,1)}), bf16[8,40,896]{2,1,0:T(8,128)(2,1)S(1)}, u32[]{:S(2)}, u32[]{:S(2)}) async-start(bf16[8,40,896]{2,1,0:T(8,128)(2,1)} %pad_maximum_fusion.3), calls=%async_computation.1 | async-start | bytes 1146880 | tf_op jit(solution)/shard_map/all_to_all | solution.py:326
  37.0 8.3 %all-to-all-done.1 = bf16[8,40,896]{2,1,0:T(8,128)(2,1)S(1)} async-done(((bf16[8,40,896]{2,1,0:T(8,128)(2,1)}), bf16[8,40,896]{2,1,0:T(8,128)(2,1)S(1)}, u32[]{:S(2)}, u32[]{:S(2)}) %all-to-all-start.1) | async-done | bytes 573472 | tf_op jit(solution)/shard_map/all_to_all | solution.py:326
  45.3 21.0 %all_gather.15 = bf16[1280,384]{1,0:T(8,128)(2,1)S(1)} all-gather(bf16[320,384]{1,0:T(8,128)(2,1)S(1)} %bitcast.231), channel_id=1, replica_groups={{0,8,16,24},{1,9,17,25},{2,10,18,26},{3,11,19,27},{4,12,20,28},{5,13,21..., dimensions={0}, use_global_device_ids=true | all-gather | bytes 1228800 | tf_op jit(solution)/shard_map/all_gather | solution.py:330
  75.3 14.2 %all_gather.16 = bf16[128,1024]{1,0:T(8,128)(2,1)S(1)} all-gather(bf16[32,1024]{1,0:T(8,128)(2,1)S(1)} %copy-done.26), channel_id=1, replica_groups={{0,8,16,24},{1,9,17,25},{2,10,18,26},{3,11,19,27},{4,12,20,28},{5,13,21..., dimensions={0}, use_global_device_ids=true | all-gather | bytes 327680 | tf_op jit(solution)/shard_map/all_gather | solution.py:330
  90.4 3.9 %all-to-all-start.2 = ((bf16[8,32,1024]{2,1,0:T(8,128)(2,1)}), bf16[8,32,1024]{2,1,0:T(8,128)(2,1)S(1)}, u32[]{:S(2)}, u32[]{:S(2)}) async-start(bf16[8,32,1024]{2,1,0:T(8,128)(2,1)} %bitcast.26), calls=%async_computation.2 | async-start | bytes 1048576 | tf_op jit(solution)/shard_map/all_to_all | solution.py:326
  97.3 8.6 %shard_map.254 = bf16[8,128,128]{2,1,0:T(8,128)(2,1)} custom-call(s32[1]{0:T(128)} %bitcast.core_ref, bf16[8,128,384]{2,1,0:T(8,128)(2,1)} %bitcast.186, bf16[12,128,256]{2,1,0:T(8,128)(2,1)} %pad_maximum_fusion.2.kv_ref, s32[8,128,1]{2,1,0:T(8,128)} %copy.48.start_ref), custom_call_target="tpu_custom_call" | custom-call | tf_op jit(solution)/shard_map/pallas_call | solution.py:428
  114.1 4.2 %all-to-all-start.3 = ((bf16[4,128,1024]{2,1,0:T(8,128)(2,1)}), bf16[4,128,1024]{2,1,0:T(8,128)(2,1)S(1)}, u32[]{:S(2)}, u32[]{:S(2)}) async-start(bf16[4,128,1024]{2,1,0:T(8,128)(2,1)} %bitcast.201), calls=%async_computation.3 | async-start | bytes 2097152 | tf_op jit(solution)/shard_map/all_to_all | solution.py:294
  119.0 13.3 %all-to-all-done.3 = bf16[4,128,1024]{2,1,0:T(8,128)(2,1)S(1)} async-done(((bf16[4,128,1024]{2,1,0:T(8,128)(2,1)}), bf16[4,128,1024]{2,1,0:T(8,128)(2,1)S(1)}, u32[]{:S(2)}, u32[]{:S(2)}) %all-to-all-start.3) | async-done | bytes 1048608 | tf_op jit(solution)/shard_map/all_to_all | solution.py:294
  134.2 4.4 %all-to-all-start.4 = ((bf16[4,128,1024]{2,1,0:T(8,128)(2,1)}), bf16[4,128,1024]{2,1,0:T(8,128)(2,1)}, u32[]{:S(2)}, u32[]{:S(2)}) async-start(bf16[4,128,1024]{2,1,0:T(8,128)(2,1)} %broadcast_in_dim.42), calls=%async_computation.4 | async-start | bytes 2097152 | tf_op jit(solution)/shard_map/all_to_all | solution.py:294
  138.6 13.1 %all-to-all-done.4 = bf16[4,128,1024]{2,1,0:T(8,128)(2,1)} async-done(((bf16[4,128,1024]{2,1,0:T(8,128)(2,1)}), bf16[4,128,1024]{2,1,0:T(8,128)(2,1)}, u32[]{:S(2)}, u32[]{:S(2)}) %all-to-all-start.4) | async-done | bytes 1048608 | tf_op jit(solution)/shard_map/all_to_all | solution.py:294
  154.7 3.6 %multiply_convert_fusion.1 = (bf16[512,512]{1,0:T(8,128)(2,1)}, f32[512,512]{1,0:T(8,128)}) fusion(f32[512]{0:T(512)S(1)} %bitcast.246, bf16[512,1024]{1,0:T(8,128)(2,1)} %bitcast.30, bf16[1024,512]{1,0:T(8,128)(2,1)} %all-gather.4.cloned.1.call-done), kind=kOutput, calls=%fused_computation.61 | convolution fusion | flops 539492352 | bytes 3672064 | tf_op jit(solution)/shard_map/dot_general | solution.py:256
  158.3 10.3 %all-gather.8.cloned.1.call-done = bf16[512,1024]{1,0:T(8,128)(2,1)} async-done(((bf16[128,1024]{1,0:T(8,128)(2,1)}), bf16[512,1024]{1,0:T(8,128)(2,1)}) %all-gather.8.cloned.1.call-update) | async-done | bytes 1048592 | tf_op jit(solution)/shard_map/all_gather | solution.py:330
  168.6 3.2 fusion.42
  181.7 4.2 %all-to-all-start.5 = ((bf16[4,128,1024]{2,1,0:T(8,128)(2,1)}), bf16[4,128,1024]{2,1,0:T(8,128)(2,1)}, u32[]{:S(2)}, u32[]{:S(2)}) async-start(bf16[4,128,1024]{2,1,0:T(8,128)(2,1)} %bitcast.202), calls=%async_computation.5 | async-start | bytes 2097152 | tf_op jit(solution)/shard_map/all_to_all | solution.py:294
  191.7 8.5 %all-to-all-done.5 = bf16[4,128,1024]{2,1,0:T(8,128)(2,1)} async-done(((bf16[4,128,1024]{2,1,0:T(8,128)(2,1)}), bf16[4,128,1024]{2,1,0:T(8,128)(2,1)}, u32[]{:S(2)}, u32[]{:S(2)}) %all-to-all-start.5) | async-done | bytes 1048608 | tf_op jit(solution)/shard_map/all_to_all | solution.py:294
  205.3 3.5 %all-to-all-start.6 = ((bf16[4,128,1024]{2,1,0:T(8,128)(2,1)}), bf16[4,128,1024]{2,1,0:T(8,128)(2,1)S(1)}, u32[]{:S(2)}, u32[]{:S(2)}) async-start(bf16[4,128,1024]{2,1,0:T(8,128)(2,1)} %broadcast_in_dim.43), calls=%async_computation.6 | async-start | bytes 2097152 | tf_op jit(solution)/shard_map/all_to_all | solution.py:294
  209.1 3.1 convolution_convert_fusion.1
  217.3 4.8 %all-to-all-done.6 = bf16[4,128,1024]{2,1,0:T(8,128)(2,1)S(1)} async-done(((bf16[4,128,1024]{2,1,0:T(8,128)(2,1)}), bf16[4,128,1024]{2,1,0:T(8,128)(2,1)S(1)}, u32[]{:S(2)}, u32[]{:S(2)}) %all-to-all-start.6) | async-done | bytes 1048608 | tf_op jit(solution)/shard_map/all_to_all | solution.py:294
  222.8 3.4 %add_convert_fusion.1 = bf16[512,1024]{1,0:T(8,128)(2,1)} fusion(bf16[512,1024]{1,0:T(8,128)(2,1)} %collective-permute-done.6, bf16[512,512]{1,0:T(8,128)(2,1)} %get-tuple-element.45, bf16[512,1024]{1,0:T(8,128)(2,1)} %all-gather.8.cloned.1.call-done), kind=kOutput, calls=%fused_computation.21 | convolution fusion | flops 538443776 | bytes 3670016 | tf_op jit(solution)/shard_map/dot_general | solution.py:256
  229.0 11.5 %shard_map.255 = (f32[8,128,128]{2,1,0:T(8,128)}, f32[12,128,256]{2,1,0:T(8,128)}) custom-call(s32[1]{0:T(128)} %bitcast.core_ref, bf16[8,128,384]{2,1,0:T(8,128)(2,1)} %bitcast.187, bf16[12,128,256]{2,1,0:T(8,128)(2,1)} %pad_maximum_fusion.2.kv_ref, s32[8,128,1]{2,1,0:T(8,128)} %copy.48.start_ref, bf16[8,128,128]{2,1,0:T(8,128)(2,1)} %bitcast.222), custom_call_target="tpu_custom_call" | custom-call | tf_op jit(solution)/shard_map/pallas_call | solution.py:428
  248.7 4.1 %all-to-all-start.10 = ((bf16[8,32,1024]{2,1,0:T(8,128)(2,1)}), bf16[8,32,1024]{2,1,0:T(8,128)(2,1)}, u32[]{:S(2)}, u32[]{:S(2)}) async-start(bf16[8,32,1024]{2,1,0:T(8,128)(2,1)} %bitcast.66), calls=%async_computation.12 | async-start | bytes 1048576 | tf_op jit(solution)/shard_map/all_to_all | solution.py:326
  261.4 4.0 %fusion.37 = (f32[1024]{0:T(1024)}, f32[1024]{0:T(1024)}, bf16[512,1024]{1,0:T(8,128)(2,1)}) fusion(bf16[4,128,1024]{2,1,0:T(8,128)(2,1)} %copy-done.6, bf16[512,384]{1,0:T(8,128)(2,1)} %get-tuple-element.52, bf16[1024,384]{1,0:T(8,128)(2,1)} %bitcast.208), kind=kOutput, calls=%fused_computation.149 | convolution fusion | flops 405272576 | bytes 3284992 | tf_op jit(solution)/shard_map/dot_general | solution.py:260
  265.6 3.2 fusion.50
  268.9 3.5 %all-to-all-start.7 = ((bf16[4,128,1024]{2,1,0:T(8,128)(2,1)}), bf16[4,128,1024]{2,1,0:T(8,128)(2,1)S(1)}, u32[]{:S(2)}, u32[]{:S(2)}) async-start(bf16[4,128,1024]{2,1,0:T(8,128)(2,1)} %bitcast.225), calls=%async_computation.7 | async-start | bytes 2097152 | tf_op jit(solution)/shard_map/all_to_all | solution.py:294
  272.6 3.4 %fusion.38 = (f32[1024]{0:T(1024)S(1)}, f32[1024]{0:T(1024)S(1)}, bf16[512,1024]{1,0:T(8,128)(2,1)}) fusion(f32[512,1024]{1,0:T(8,128)} %fusion.50, bf16[4,128,1024]{2,1,0:T(8,128)(2,1)S(1)} %all-to-all-done, bf16[512,1024]{1,0:T(8,128)(2,1)} %collective-permute-done.8), kind=kLoop, calls=%fused_computation.150 | loop fusion | flops 3667968 | bytes 5251072 | tf_op jit(solution)/shard_map/reduce_sum | solution.py:627
  281.3 7.1 %collective-permute-done.10 = f32[12,1024]{1,0:T(8,128)S(1)} collective-permute-done((f32[12,1024]{1,0:T(8,128)S(1)}, f32[12,1024]{1,0:T(8,128)S(1)}, u32[]{:S(2)}, u32[]{:S(2)}) %collective-permute-start.10) | collective-permute-done | bytes 49184 | tf_op jit(solution)/shard_map/ppermute | solution.py:273
  295.3 3.6 %all-to-all-start.8 = ((bf16[4,128,1024]{2,1,0:T(8,128)(2,1)}), bf16[4,128,1024]{2,1,0:T(8,128)(2,1)S(1)}, u32[]{:S(2)}, u32[]{:S(2)}) async-start(bf16[4,128,1024]{2,1,0:T(8,128)(2,1)} %bitcast.49), calls=%async_computation.8 | async-start | bytes 2097152 | tf_op jit(solution)/shard_map/all_to_all | solution.py:294
  301.2 5.0 %collective-permute-done.13 = f32[12,1024]{1,0:T(8,128)S(1)} collective-permute-done((f32[12,1024]{1,0:T(8,128)S(1)}, f32[12,1024]{1,0:T(8,128)S(1)}, u32[]{:S(2)}, u32[]{:S(2)}) %collective-permute-start.13) | collective-permute-done | bytes 49184 | tf_op jit(solution)/shard_map/ppermute | solution.py:273
  311.2 3.5 %all-to-all-start.9 = ((bf16[8,32,896]{2,1,0:T(8,128)(2,1)}), bf16[8,32,896]{2,1,0:T(8,128)(2,1)S(1)}, u32[]{:S(2)}, u32[]{:S(2)}) async-start(bf16[8,32,896]{2,1,0:T(8,128)(2,1)} %bitcast.62), calls=%async_computation.11 | async-start | bytes 917504 | tf_op jit(solution)/shard_map/all_to_all | solution.py:326
  316.2 7.5 %all-to-all-done.9 = bf16[8,32,896]{2,1,0:T(8,128)(2,1)S(1)} async-done(((bf16[8,32,896]{2,1,0:T(8,128)(2,1)}), bf16[8,32,896]{2,1,0:T(8,128)(2,1)S(1)}, u32[]{:S(2)}, u32[]{:S(2)}) %all-to-all-start.9) | async-done | bytes 458784 | tf_op jit(solution)/shard_map/all_to_all | solution.py:326
  (293 shorter events, 106.9 us)
Async XLA Ops:
  12.5 19.0 %all-to-all-start = ((bf16[4,128,1024]{2,1,0:T(8,128)(2,1)}), bf16[4,128,1024]{2,1,0:T(8,128)(2,1)S(1)}, u32[]{:S(2)}, u32[]{:S(2)}) async-start(bf16[4,128,1024]{2,1,0:T(8,128)(2,1)} %broadcast_in_dim.36), calls=%async_computation | async-start | bytes 2097152 | tf_op jit(solution)/shard_map/all_to_all | solution.py:294
  31.5 13.7 %all-to-all-start.1 = ((bf16[8,40,896]{2,1,0:T(8,128)(2,1)}), bf16[8,40,896]{2,1,0:T(8,128)(2,1)S(1)}, u32[]{:S(2)}, u32[]{:S(2)}) async-start(bf16[8,40,896]{2,1,0:T(8,128)(2,1)} %pad_maximum_fusion.3), calls=%async_computation.1 | async-start | bytes 1146880 | tf_op jit(solution)/shard_map/all_to_all | solution.py:326
  35.1 116.7 %all-gather.6.cloned.1.call-start = ((), (), s32[]{:S(2)}) async-start(), calls=%async_computation.16 | async-start | bytes 2359296 | tf_op jit(solution)/shard_map/all_gather | solution.py:496
  35.9 33.7 %collective-permute-start = (bf16[4,128,1024]{2,1,0:T(8,128)(2,1)S(1)}, bf16[4,128,1024]{2,1,0:T(8,128)(2,1)S(1)}, u32[]{:S(2)}, u32[]{:S(2)}) collective-permute-start(bf16[4,128,1024]{2,1,0:T(8,128)(2,1)S(1)} %all-to-all-done), channel_id=1, source_target_pairs={{0,1},{1,0},{2,3},{3,2},{4,5},{5,4},{6,7},{7,6},{8,9},{9,8},{10,11... | collective-permute-start | bytes 3145736 | tf_op jit(solution)/shard_map/ppermute | solution.py:273
  73.1 22.3 %collective-permute-start.1 = (bf16[4,128,256]{2,1,0:T(8,128)(2,1)}, bf16[4,128,256]{2,1,0:T(8,128)(2,1)}, u32[]{:S(2)}, u32[]{:S(2)}) collective-permute-start(bf16[4,128,256]{2,1,0:T(8,128)(2,1)} %bitcast.21), channel_id=1, source_target_pairs={{0,8},{1,9},{2,10},{3,11},{4,12},{5,13},{6,14},{7,15},{8,16},{9,17... | collective-permute-start | bytes 786440 | tf_op jit(solution)/shard_map/ppermute | solution.py:26
  90.4 16.6 %all-to-all-start.2 = ((bf16[8,32,1024]{2,1,0:T(8,128)(2,1)}), bf16[8,32,1024]{2,1,0:T(8,128)(2,1)S(1)}, u32[]{:S(2)}, u32[]{:S(2)}) async-start(bf16[8,32,1024]{2,1,0:T(8,128)(2,1)} %bitcast.26), calls=%async_computation.2 | async-start | bytes 1048576 | tf_op jit(solution)/shard_map/all_to_all | solution.py:326
  94.2 60.5 %all-gather.4.cloned.1.call-start = ((), (), s32[]{:S(2)}) async-start(), calls=%async_computation.15 | async-start | bytes 1310720 | tf_op jit(solution)/shard_map/all_gather | solution.py:330
  108.4 3.1 collective-permute-start.2
  114.1 18.2 %all-to-all-start.3 = ((bf16[4,128,1024]{2,1,0:T(8,128)(2,1)}), bf16[4,128,1024]{2,1,0:T(8,128)(2,1)S(1)}, u32[]{:S(2)}, u32[]{:S(2)}) async-start(bf16[4,128,1024]{2,1,0:T(8,128)(2,1)} %bitcast.201), calls=%async_computation.3 | async-start | bytes 2097152 | tf_op jit(solution)/shard_map/all_to_all | solution.py:294
  118.3 50.3 %all-gather.8.cloned.1.call-start = ((), (), s32[]{:S(2)}) async-start(), calls=%async_computation.17 | async-start | bytes 1310720 | tf_op jit(solution)/shard_map/all_gather | solution.py:330
  134.2 17.6 %all-to-all-start.4 = ((bf16[4,128,1024]{2,1,0:T(8,128)(2,1)}), bf16[4,128,1024]{2,1,0:T(8,128)(2,1)}, u32[]{:S(2)}, u32[]{:S(2)}) async-start(bf16[4,128,1024]{2,1,0:T(8,128)(2,1)} %broadcast_in_dim.42), calls=%async_computation.4 | async-start | bytes 2097152 | tf_op jit(solution)/shard_map/all_to_all | solution.py:294
  151.8 20.7 %collective-permute-start.3 = (bf16[4,128,1024]{2,1,0:T(8,128)(2,1)}, bf16[4,128,1024]{2,1,0:T(8,128)(2,1)}, u32[]{:S(2)}, u32[]{:S(2)}) collective-permute-start(bf16[4,128,1024]{2,1,0:T(8,128)(2,1)} %all-to-all-done.4), channel_id=1, source_target_pairs={{0,1},{1,0},{2,3},{3,2},{4,5},{5,4},{6,7},{7,6},{8,9},{9,8},{10,11... | collective-permute-start | bytes 3145736 | tf_op jit(solution)/shard_map/ppermute | solution.py:273
  177.6 2.7 collective-permute-start.4
  181.7 18.5 %all-to-all-start.5 = ((bf16[4,128,1024]{2,1,0:T(8,128)(2,1)}), bf16[4,128,1024]{2,1,0:T(8,128)(2,1)}, u32[]{:S(2)}, u32[]{:S(2)}) async-start(bf16[4,128,1024]{2,1,0:T(8,128)(2,1)} %bitcast.202), calls=%async_computation.5 | async-start | bytes 2097152 | tf_op jit(solution)/shard_map/all_to_all | solution.py:294
  186.0 93.6 %reduce-scatter.11.cloned.1.call-start = ((), (), s32[]{:S(2)}) async-start(), calls=%async_computation.21 | async-start | bytes 1310720 | tf_op jit(solution)/shard_map/reduce_scatter | solution.py:334
  205.3 16.9 %all-to-all-start.6 = ((bf16[4,128,1024]{2,1,0:T(8,128)(2,1)}), bf16[4,128,1024]{2,1,0:T(8,128)(2,1)S(1)}, u32[]{:S(2)}, u32[]{:S(2)}) async-start(bf16[4,128,1024]{2,1,0:T(8,128)(2,1)} %broadcast_in_dim.43), calls=%async_computation.6 | async-start | bytes 2097152 | tf_op jit(solution)/shard_map/all_to_all | solution.py:294
  208.8 99.2 %reduce-scatter.7.cloned.1.call-start = ((), (), s32[]{:S(2)}) async-start(), calls=%async_computation.19 | async-start | bytes 1310720 | tf_op jit(solution)/shard_map/reduce_scatter | solution.py:334
  212.2 10.6 %collective-permute-start.6 = (bf16[512,1024]{1,0:T(8,128)(2,1)}, bf16[512,1024]{1,0:T(8,128)(2,1)}, u32[]{:S(2)}, u32[]{:S(2)}) collective-permute-start(bf16[512,1024]{1,0:T(8,128)(2,1)} %convolution_convert_fusion.1), channel_id=1, source_target_pairs={{0,1},{1,0},{2,3},{3,2},{4,5},{5,4},{6,7},{7,6},{8,9},{9,8},{10,11... | collective-permute-start | bytes 3145736 | tf_op jit(solution)/shard_map/ppermute | solution.py:273
  222.1 4.5 %collective-permute-start.5 = (bf16[4,128,1024]{2,1,0:T(8,128)(2,1)S(1)}, bf16[4,128,1024]{2,1,0:T(8,128)(2,1)}, u32[]{:S(2)}, u32[]{:S(2)}) collective-permute-start(bf16[4,128,1024]{2,1,0:T(8,128)(2,1)S(1)} %all-to-all-done.6), channel_id=1, source_target_pairs={{0,1},{1,0},{2,3},{3,2},{4,5},{5,4},{6,7},{7,6},{8,9},{9,8},{10,11... | collective-permute-start | bytes 3145736 | tf_op jit(solution)/shard_map/ppermute | solution.py:273
  244.6 10.9 %collective-permute-start.7 = (bf16[4,128,256]{2,1,0:T(8,128)(2,1)}, bf16[4,128,256]{2,1,0:T(8,128)(2,1)}, u32[]{:S(2)}, u32[]{:S(2)}) collective-permute-start(bf16[4,128,256]{2,1,0:T(8,128)(2,1)} %slice.203), channel_id=1, source_target_pairs={{8,0},{9,1},{10,2},{11,3},{12,4},{13,5},{14,6},{15,7},{16,8},{17,9... | collective-permute-start | bytes 786440 | tf_op jit(solution)/shard_map/ppermute | solution.py:26
  248.7 20.2 %all-to-all-start.10 = ((bf16[8,32,1024]{2,1,0:T(8,128)(2,1)}), bf16[8,32,1024]{2,1,0:T(8,128)(2,1)}, u32[]{:S(2)}, u32[]{:S(2)}) async-start(bf16[8,32,1024]{2,1,0:T(8,128)(2,1)} %bitcast.66), calls=%async_computation.12 | async-start | bytes 1048576 | tf_op jit(solution)/shard_map/all_to_all | solution.py:326
  252.8 55.2 %reduce-scatter.5.cloned.1.call-start = ((), (), s32[]{:S(2)}) async-start(), calls=%async_computation.18 | async-start | bytes 983040 | tf_op jit(solution)/shard_map/reduce_scatter | solution.py:334
  265.4 7.2 %collective-permute-start.8 = (bf16[512,1024]{1,0:T(8,128)(2,1)}, bf16[512,1024]{1,0:T(8,128)(2,1)}, u32[]{:S(2)}, u32[]{:S(2)}) collective-permute-start(bf16[512,1024]{1,0:T(8,128)(2,1)} %get-tuple-element.71), channel_id=1, source_target_pairs={{0,1},{1,0},{2,3},{3,2},{4,5},{5,4},{6,7},{7,6},{8,9},{9,8},{10,11... | collective-permute-start | bytes 3145736 | tf_op jit(solution)/shard_map/ppermute | solution.py:273
  268.9 25.4 %all-to-all-start.7 = ((bf16[4,128,1024]{2,1,0:T(8,128)(2,1)}), bf16[4,128,1024]{2,1,0:T(8,128)(2,1)S(1)}, u32[]{:S(2)}, u32[]{:S(2)}) async-start(bf16[4,128,1024]{2,1,0:T(8,128)(2,1)} %bitcast.225), calls=%async_computation.7 | async-start | bytes 2097152 | tf_op jit(solution)/shard_map/all_to_all | solution.py:294
  272.4 52.5 %reduce-scatter.9.cloned.1.call-start = ((), (), s32[]{:S(2)}) async-start(), calls=%async_computation.20 | async-start | bytes 327680 | tf_op jit(solution)/shard_map/reduce_scatter | solution.py:334
  276.1 1.5 collective-permute-start.9
  277.6 10.8 %collective-permute-start.10 = (f32[12,1024]{1,0:T(8,128)S(1)}, f32[12,1024]{1,0:T(8,128)S(1)}, u32[]{:S(2)}, u32[]{:S(2)}) collective-permute-start(f32[12,1024]{1,0:T(8,128)S(1)} %add.349), channel_id=1, source_target_pairs={{0,2},{1,3},{2,0},{3,1},{4,6},{5,7},{6,4},{7,5},{8,10},{9,11},{10,... | collective-permute-start | bytes 147464 | tf_op jit(solution)/shard_map/ppermute | solution.py:273
  288.4 4.3 %collective-permute-start.11 = (f32[12,1024]{1,0:T(8,128)S(1)}, f32[12,1024]{1,0:T(8,128)S(1)}, u32[]{:S(2)}, u32[]{:S(2)}) collective-permute-start(f32[12,1024]{1,0:T(8,128)S(1)} %add.350), channel_id=1, source_target_pairs={{0,4},{1,5},{2,6},{3,7},{4,0},{5,1},{6,2},{7,3},{8,12},{9,13},{10,... | collective-permute-start | bytes 147464 | tf_op jit(solution)/shard_map/ppermute | solution.py:273
  292.7 6.2 %collective-permute-start.12 = (f32[12,1024]{1,0:T(8,128)S(1)}, f32[12,1024]{1,0:T(8,128)S(1)}, u32[]{:S(2)}, u32[]{:S(2)}) collective-permute-start(f32[12,1024]{1,0:T(8,128)S(1)} %add.351), channel_id=1, source_target_pairs={{0,8},{1,9},{2,10},{3,11},{4,12},{5,13},{6,14},{7,15},{8,0},{9,1},... | collective-permute-start | bytes 147464 | tf_op jit(solution)/shard_map/ppermute | solution.py:273
  295.3 15.9 %all-to-all-start.8 = ((bf16[4,128,1024]{2,1,0:T(8,128)(2,1)}), bf16[4,128,1024]{2,1,0:T(8,128)(2,1)S(1)}, u32[]{:S(2)}, u32[]{:S(2)}) async-start(bf16[4,128,1024]{2,1,0:T(8,128)(2,1)} %bitcast.49), calls=%async_computation.8 | async-start | bytes 2097152 | tf_op jit(solution)/shard_map/all_to_all | solution.py:294
  299.0 7.2 %collective-permute-start.13 = (f32[12,1024]{1,0:T(8,128)S(1)}, f32[12,1024]{1,0:T(8,128)S(1)}, u32[]{:S(2)}, u32[]{:S(2)}) collective-permute-start(f32[12,1024]{1,0:T(8,128)S(1)} %add.352), channel_id=1, source_target_pairs={{0,16},{1,17},{2,18},{3,19},{4,20},{5,21},{6,22},{7,23},{8,24},{9,... | collective-permute-start | bytes 147464 | tf_op jit(solution)/shard_map/ppermute | solution.py:273
  311.2 12.4 %all-to-all-start.9 = ((bf16[8,32,896]{2,1,0:T(8,128)(2,1)}), bf16[8,32,896]{2,1,0:T(8,128)(2,1)S(1)}, u32[]{:S(2)}, u32[]{:S(2)}) async-start(bf16[8,32,896]{2,1,0:T(8,128)(2,1)} %bitcast.62), calls=%async_computation.11 | async-start | bytes 917504 | tf_op jit(solution)/shard_map/all_to_all | solution.py:326
  (51 other events, 351.1 us)
Sparse Core Ops, SparseCore 0:
  45.4 27.1 all-gather.5
  109.7 29.8 all-gather.3
  141.2 27.3 all-gather.7
  189.8 27.1 reduce-scatter.10
  222.3 25.9 reduce-scatter.6
  265.7 23.2 reduce-scatter.4
  291.8 19.4 reduce-scatter.8
